TPU v7x, 32 devices: a whole 2x2x4 slice. The times are simulated.
32 devices in a mesh: row: 4 (over z), col: 8 (over y, x, core).
Axes of the slice: x: 2, y: 2, z: 4, core: 2. Of those that a mesh axis runs over, the one named last changes fastest.
Arguments:
- symmetric: float32 [16384, 16384], P('row', 'col'), may hold values from -8 to 8, as said below
- reflectors: float32 [4, 64, 16384], P(None, None, ('row', 'col')), may hold values from -0.125 to 0.125
- tri_factor: float32 [4, 64, 64], replicated, may hold values from -0.4 to 1.5, as said below
Outputs:
- updated: float32 [16384, 16384], P('row', 'col')
Inputs may be any that keep to these rules, and one draw needn't show every extreme that they name: symmetric is a symmetric matrix. Each tri_factor[p] is upper triangular.
All inputs are finite; a program needn't handle non-finite values.
Results may differ from a plain program's by a relative error of at most 0.00029.
Values sent between devices are 32-bit elements; how exact they have to be, the bound alone decides.
No kernel may reach another device: no remote copies, remote signals or barrier semaphores. Data moves between devices by JAX's collectives and lax.ppermute only.
A program may use at most 128 MiB of HBM per device.

v0:
```python
import jax
import jax.numpy as jnp
from jax import lax
from jax.sharding import PartitionSpec as P


def broadcast(value, axis, source):
    kept = jnp.where(lax.axis_index(axis) == source, value, 0).astype(value.dtype)
    return lax.psum(kept, axis)


def shards(symmetric, reflectors, tri_factor):
    highest = lax.Precision.HIGHEST
    cols_here = symmetric.shape[1]
    row_count = lax.axis_size("row")
    col_count = lax.axis_size("col")
    col_index = lax.axis_index("col")
    owner = col_index * row_count // col_count
    offset = col_index % (col_count // row_count) * cols_here
    matrix = symmetric
    for panel in range(reflectors.shape[0]):
        piece = reflectors[panel]
        factor = tri_factor[panel]
        reflect_rows = lax.all_gather(piece, "col", axis=1, tiled=True)
        reflect_cols = broadcast(
            lax.dynamic_slice_in_dim(reflect_rows, offset, cols_here, 1), "row", owner
        )
        partial_value = lax.dot_general(
            reflect_cols,
            matrix,
            (((1,), (1,)), ((), ())),
            precision=highest,
            preferred_element_type=jnp.float32,
        )
        product_rows = lax.psum(partial_value, "col")
        image_rows = jnp.dot(
            factor.T, product_rows, precision=highest, preferred_element_type=jnp.float32
        )
        local_inner = lax.dot_general(
            reflect_rows,
            image_rows,
            (((1,), (1,)), ((), ())),
            precision=highest,
            preferred_element_type=jnp.float32,
        )
        inner = lax.psum(local_inner, "row")
        coupling = jnp.dot(factor.T, inner, precision=highest, preferred_element_type=jnp.float32)
        update_rows = image_rows - 0.5 * jnp.dot(
            coupling.T, reflect_rows, precision=highest, preferred_element_type=jnp.float32
        )
        update_cols = broadcast(
            lax.dynamic_slice_in_dim(update_rows, offset, cols_here, 1), "row", owner
        )
        left_block = jnp.concatenate([reflect_rows, update_rows], axis=0)
        right_block = jnp.concatenate([update_cols, reflect_cols], axis=0)
        matrix = matrix - lax.dot_general(
            left_block,
            right_block,
            (((0,), (0,)), ((), ())),
            precision=highest,
            preferred_element_type=jnp.float32,
        )
    return matrix


def solution(mesh):
    placed = (P("row", "col"), P(None, None, ("row", "col")), P())
    return jax.shard_map(
        shards, mesh=mesh, in_specs=placed, out_specs=P("row", "col"), check_vma=False
    )
```

profile of v0, /device:TPU:0, one launch (start us, length us, event | category | flops | bytes accessed | tf_op | source)
XLA Modules:
  0.0 874.3 jit_solution(7085528150204027778)
XLA Ops:
  6.5 1.9 fusion.64
  8.6 26.8 %all-gather.9.cloned.1.call-done = f32[1,64,4096]{2,1,0:T(8,128)} async-done(((f32[1,64,512]{2,1,0:T(8,128)}), f32[1,64,4096]{2,1,0:T(8,128)}) %all-gather.9.cloned.1.call-update) | async-done | bytes 1048592 | tf_op jit(solution)/shard_map/all_gather | solution.py:24
  35.4 2.0 select_bitcast_fusion.3
  38.1 38.2 %all-reduce.13.cloned.1.call-done = f32[64,2048]{1,0:T(8,128)} async-done(((f32[64,2048]{1,0:T(8,128)}), f32[64,2048]{1,0:T(8,128)}) %all-reduce.13.cloned.1.call-update) | async-done | bytes 524304 | tf_op jit(solution)/shard_map/psum | solution.py:9
  76.4 38.3 %fusion.65 = f32[64,4096]{1,0:T(8,128)} fusion(f32[64,2048]{1,0:T(8,128)} %all-reduce.13.cloned.1.call-done, f32[4096,2048]{1,0:T(8,128)} %param.3), kind=kOutput, calls=%fused_computation.85 | convolution fusion | flops 6442450944 | bytes 35127296 | tf_op jit(solution)/shard_map/dot_general | solution.py:28
  114.9 1.9 select_bitcast_fusion.2
  116.8 54.5 %all-reduce.15.cloned.1.call-done = f32[64,4096]{1,0:T(8,128)} async-done(((f32[64,4096]{1,0:T(8,128)}), f32[64,4096]{1,0:T(8,128)}) %all-reduce.15.cloned.1.call-update) | async-done | bytes 1048592 | tf_op jit(solution)/shard_map/psum | solution.py:35
  171.3 2.3 fusion.42
  174.6 18.9 %psum.114 = f32[64,64]{0,1:T(8,128)S(1)} all-reduce(f32[64,64]{0,1:T(8,128)S(1)} %convolution_bitcast_fusion.3), channel_id=1, replica_groups=mesh['row'=4,'col'=8] {'row'}, use_global_device_ids=true, to_apply=%region_2.3 | all-reduce | flops 4096 | bytes 32768 | tf_op jit(solution)/shard_map/psum | solution.py:46
  193.7 1.0 fusion.3
  196.2 48.1 %all-reduce.29.cloned.1.call-done = (f32[64,2048]{1,0:T(8,128)}, f32[64,2048]{1,0:T(8,128)}) async-done(((f32[64,2048]{1,0:T(8,128)}, f32[64,2048]{1,0:T(8,128)}), (f32[64,2048]{1,0:T(8,128)}, f32[64,2048]{1,0:T(8,128)})) %all-reduce.29.cloned.1.call-update) | async-done | bytes 1048592 | tf_op jit(solution)/shard_map/psum | solution.py:9
  244.3 34.7 %convolution_subtract_fusion.3 = f32[4096,2048]{1,0:T(8,128)} fusion(f32[4096,2048]{1,0:T(8,128)} %param.3, f32[64,4096]{1,0:T(8,128)S(1)} %fusion.3, f32[64,4096]{1,0:T(8,128)S(1)} %bitcast.88, f32[64,2048]{1,0:T(8,128)} %all-reduce.13.cloned.1.call-done, f32[64,2048]{1,0:T(8,128)} %get-tuple-element.9), kind=kOutput, calls=%fused_computation.3 | convolution fusion | flops 12894076928 | bytes 70254592 | tf_op jit(solution)/shard_map/dot_general | solution.py:56
  279.0 36.5 %fusion.66 = f32[64,4096]{1,0:T(8,128)} fusion(f32[64,2048]{1,0:T(8,128)S(1)} %copy-done.4, f32[4096,2048]{1,0:T(8,128)} %convolution_subtract_fusion.3), kind=kOutput, calls=%fused_computation.86 | convolution fusion | flops 6442450944 | bytes 35127296 | tf_op jit(solution)/shard_map/dot_general | solution.py:28
  315.6 1.9 select_bitcast_fusion.1
  317.5 54.1 %all-reduce.17.cloned.1.call-done = f32[64,4096]{1,0:T(8,128)} async-done(((f32[64,4096]{1,0:T(8,128)}), f32[64,4096]{1,0:T(8,128)}) %all-reduce.17.cloned.1.call-update) | async-done | bytes 1048592 | tf_op jit(solution)/shard_map/psum | solution.py:35
  371.6 2.3 fusion.38
  374.9 18.9 %psum.118 = f32[64,64]{0,1:T(8,128)S(1)} all-reduce(f32[64,64]{0,1:T(8,128)S(1)} %convolution_bitcast_fusion.2), channel_id=1, replica_groups=mesh['row'=4,'col'=8] {'row'}, use_global_device_ids=true, to_apply=%region_6.7 | all-reduce | flops 4096 | bytes 32768 | tf_op jit(solution)/shard_map/psum | solution.py:46
  396.7 47.9 %all-reduce.27.cloned.1.call-done = (f32[64,2048]{1,0:T(8,128)}, f32[64,2048]{1,0:T(8,128)}) async-done(((f32[64,2048]{1,0:T(8,128)}, f32[64,2048]{1,0:T(8,128)}), (f32[64,2048]{1,0:T(8,128)}, f32[64,2048]{1,0:T(8,128)})) %all-reduce.27.cloned.1.call-update) | async-done | bytes 1048592 | tf_op jit(solution)/shard_map/psum | solution.py:9
  444.6 35.0 %convolution_subtract_fusion.2 = f32[4096,2048]{1,0:T(8,128)} fusion(f32[4096,2048]{1,0:T(8,128)} %convolution_subtract_fusion.3, f32[64,4096]{1,0:T(8,128)S(1)} %fusion.2, f32[64,4096]{1,0:T(8,128)S(1)} %bitcast.90, f32[64,2048]{1,0:T(8,128)} %get-tuple-element.10, f32[64,2048]{1,0:T(8,128)} %get-tuple-element.7), kind=kOutput, calls=%fused_computation.2 | convolution fusion | flops 12894076928 | bytes 70254592 | tf_op jit(solution)/shard_map/dot_general | solution.py:56
  479.6 36.5 %fusion.67 = f32[64,4096]{1,0:T(8,128)} fusion(f32[64,2048]{1,0:T(8,128)S(1)} %copy-done.5, f32[4096,2048]{1,0:T(8,128)} %convolution_subtract_fusion.2), kind=kOutput, calls=%fused_computation.87 | convolution fusion | flops 6442450944 | bytes 35127296 | tf_op jit(solution)/shard_map/dot_general | solution.py:28
  516.2 1.9 select_bitcast_fusion
  518.1 54.1 %all-reduce.19.cloned.1.call-done = f32[64,4096]{1,0:T(8,128)} async-done(((f32[64,4096]{1,0:T(8,128)}), f32[64,4096]{1,0:T(8,128)}) %all-reduce.19.cloned.1.call-update) | async-done | bytes 1048592 | tf_op jit(solution)/shard_map/psum | solution.py:35
  572.2 2.3 fusion.34
  575.5 18.9 %psum.122 = f32[64,64]{0,1:T(8,128)S(1)} all-reduce(f32[64,64]{0,1:T(8,128)S(1)} %convolution_bitcast_fusion.1), channel_id=1, replica_groups=mesh['row'=4,'col'=8] {'row'}, use_global_device_ids=true, to_apply=%region_10.11 | all-reduce | flops 4096 | bytes 32768 | tf_op jit(solution)/shard_map/psum | solution.py:46
  596.5 48.6 %all-reduce.25.cloned.1.call-done = (f32[64,2048]{1,0:T(8,128)}, f32[64,2048]{1,0:T(8,128)}) async-done(((f32[64,2048]{1,0:T(8,128)}, f32[64,2048]{1,0:T(8,128)}), (f32[64,2048]{1,0:T(8,128)}, f32[64,2048]{1,0:T(8,128)})) %all-reduce.25.cloned.1.call-update) | async-done | bytes 1048592 | tf_op jit(solution)/shard_map/psum | solution.py:9
  645.2 34.8 %convolution_subtract_fusion.1 = f32[4096,2048]{1,0:T(8,128)} fusion(f32[4096,2048]{1,0:T(8,128)} %convolution_subtract_fusion.2, f32[64,4096]{1,0:T(8,128)S(1)} %fusion.1, f32[64,4096]{1,0:T(8,128)S(1)} %bitcast.89, f32[64,2048]{1,0:T(8,128)} %get-tuple-element.8, f32[64,2048]{1,0:T(8,128)} %get-tuple-element.5), kind=kOutput, calls=%fused_computation.1 | convolution fusion | flops 12894076928 | bytes 70254592 | tf_op jit(solution)/shard_map/dot_general | solution.py:56
  680.0 36.5 %fusion.68 = f32[64,4096]{1,0:T(8,128)} fusion(f32[64,2048]{1,0:T(8,128)S(1)} %copy-done.6, f32[4096,2048]{1,0:T(8,128)} %convolution_subtract_fusion.1), kind=kOutput, calls=%fused_computation.88 | convolution fusion | flops 6442450944 | bytes 35127296 | tf_op jit(solution)/shard_map/dot_general | solution.py:28
  716.6 56.0 %all-reduce.21.cloned.1.call-done = f32[64,4096]{1,0:T(8,128)} async-done(((f32[64,4096]{1,0:T(8,128)}), f32[64,4096]{1,0:T(8,128)}) %all-reduce.21.cloned.1.call-update) | async-done | bytes 1048592 | tf_op jit(solution)/shard_map/psum | solution.py:35
  772.6 2.3 fusion.30
  775.9 19.3 %psum.126 = f32[64,64]{0,1:T(8,128)S(1)} all-reduce(f32[64,64]{0,1:T(8,128)S(1)} %convolution_bitcast_fusion), channel_id=1, replica_groups=mesh['row'=4,'col'=8] {'row'}, use_global_device_ids=true, to_apply=%region_14.15 | all-reduce | flops 4096 | bytes 32768 | tf_op jit(solution)/shard_map/psum | solution.py:46
  797.2 35.4 %all-reduce.23.cloned.1.call-done = f32[64,2048]{1,0:T(8,128)} async-done(((f32[64,2048]{1,0:T(8,128)}), f32[64,2048]{1,0:T(8,128)}) %all-reduce.23.cloned.1.call-update) | async-done | bytes 524304 | tf_op jit(solution)/shard_map/psum | solution.py:9
  832.7 34.6 %convolution_subtract_fusion = f32[4096,2048]{1,0:T(8,128)} fusion(f32[4096,2048]{1,0:T(8,128)} %convolution_subtract_fusion.1, f32[64,4096]{1,0:T(8,128)S(1)} %fusion, f32[64,4096]{1,0:T(8,128)S(1)} %bitcast.91, f32[64,2048]{1,0:T(8,128)} %get-tuple-element.6, f32[64,2048]{1,0:T(8,128)} %all-reduce.23.cloned.1.call-done), kind=kOutput, calls=%fused_computation | convolution fusion | flops 12894076928 | bytes 70254592 | tf_op jit(solution)/shard_map/dot_general | solution.py:56
  (60 shorter events, 13.8 us)
Async XLA Ops:
  6.5 164.8 %copy-start.7 = (f32[4,64,64]{2,1,0:T(8,128)S(1)}, f32[4,64,64]{2,1,0:T(8,128)}, u32[]{:S(2)}) copy-start(f32[4,64,64]{2,1,0:T(8,128)} %param.5) | copy-start | bytes 196612
  6.5 28.8 %all-gather.9.cloned.1.call-start = ((), (), s32[]{:S(2)}) async-start(), calls=%async_computation.6 | async-start | bytes 1179648 | tf_op jit(solution)/shard_map/all_gather | solution.py:24
  8.5 67.9 %all-reduce.13.cloned.1.call-start = ((), (), s32[]{:S(2)}) async-start(), calls=%async_computation | async-start | bytes 1048576 | tf_op jit(solution)/shard_map/psum | solution.py:9
  35.4 138.2 %copy-start = (f32[1,64,4096]{2,1,0:T(8,128)S(1)}, f32[1,64,4096]{2,1,0:T(8,128)}, u32[]{:S(2)}) copy-start(f32[1,64,4096]{2,1,0:T(8,128)} %all-gather.9.cloned.1.call-done) | copy-start | bytes 3145732
  37.4 77.5 %all-gather.11.cloned.1.call-start = ((), (), s32[]{:S(2)}) async-start(), calls=%async_computation.7 | async-start | bytes 1179648 | tf_op jit(solution)/shard_map/all_gather | solution.py:24
  38.1 133.2 %all-reduce.15.cloned.1.call-start = ((), (), s32[]{:S(2)}) async-start(), calls=%async_computation.1 | async-start | bytes 2097152 | tf_op jit(solution)/shard_map/psum | solution.py:35
  114.7 129.6 %all-reduce.29.cloned.1.call-start = ((), (), s32[]{:S(2)}) async-start(), calls=%async_computation.12 | async-start | bytes 2097152 | tf_op jit(solution)/shard_map/psum | solution.py:9
  195.6 120.0 %all-gather.13.cloned.1.call-start = ((), (), s32[]{:S(2)}) async-start(), calls=%async_computation.8 | async-start | bytes 1179648 | tf_op jit(solution)/shard_map/all_gather | solution.py:24
  196.2 175.5 %all-reduce.17.cloned.1.call-start = ((), (), s32[]{:S(2)}) async-start(), calls=%async_computation.2 | async-start | bytes 2097152 | tf_op jit(solution)/shard_map/psum | solution.py:35
  244.3 34.7 %copy-start.4 = (f32[64,2048]{1,0:T(8,128)S(1)}, f32[64,2048]{1,0:T(8,128)}, u32[]{:S(2)}) copy-start(f32[64,2048]{1,0:T(8,128)} %get-tuple-element.10) | copy-start | bytes 1572868
  279.0 94.9 %copy-start.2 = (f32[1,64,4096]{2,1,0:T(8,128)S(1)}, f32[1,64,4096]{2,1,0:T(8,128)}, u32[]{:S(2)}) copy-start(f32[1,64,4096]{2,1,0:T(8,128)} %all-gather.11.cloned.1.call-done) | copy-start | bytes 3145732
  315.5 129.1 %all-reduce.27.cloned.1.call-start = ((), (), s32[]{:S(2)}) async-start(), calls=%async_computation.11 | async-start | bytes 2097152 | tf_op jit(solution)/shard_map/psum | solution.py:9
  395.9 120.3 %all-gather.15.cloned.1.call-start = ((), (), s32[]{:S(2)}) async-start(), calls=%async_computation.9 | async-start | bytes 1179648 | tf_op jit(solution)/shard_map/all_gather | solution.py:24
  396.7 175.6 %all-reduce.19.cloned.1.call-start = ((), (), s32[]{:S(2)}) async-start(), calls=%async_computation.3 | async-start | bytes 2097152 | tf_op jit(solution)/shard_map/psum | solution.py:35
  444.6 35.0 %copy-start.5 = (f32[64,2048]{1,0:T(8,128)S(1)}, f32[64,2048]{1,0:T(8,128)}, u32[]{:S(2)}) copy-start(f32[64,2048]{1,0:T(8,128)} %get-tuple-element.8) | copy-start | bytes 1572868
  479.6 94.9 %copy-start.1 = (f32[1,64,4096]{2,1,0:T(8,128)S(1)}, f32[1,64,4096]{2,1,0:T(8,128)}, u32[]{:S(2)}) copy-start(f32[1,64,4096]{2,1,0:T(8,128)} %all-gather.13.cloned.1.call-done) | copy-start | bytes 3145732
  516.1 129.0 %all-reduce.25.cloned.1.call-start = ((), (), s32[]{:S(2)}) async-start(), calls=%async_computation.10 | async-start | bytes 2097152 | tf_op jit(solution)/shard_map/psum | solution.py:9
  596.5 176.1 %all-reduce.21.cloned.1.call-start = ((), (), s32[]{:S(2)}) async-start(), calls=%async_computation.4 | async-start | bytes 2097152 | tf_op jit(solution)/shard_map/psum | solution.py:35
  645.2 34.8 %copy-start.6 = (f32[64,2048]{1,0:T(8,128)S(1)}, f32[64,2048]{1,0:T(8,128)}, u32[]{:S(2)}) copy-start(f32[64,2048]{1,0:T(8,128)} %get-tuple-element.6) | copy-start | bytes 1572868
  680.0 94.9 %copy-start.3 = (f32[1,64,4096]{2,1,0:T(8,128)S(1)}, f32[1,64,4096]{2,1,0:T(8,128)}, u32[]{:S(2)}) copy-start(f32[1,64,4096]{2,1,0:T(8,128)} %all-gather.15.cloned.1.call-done) | copy-start | bytes 3145732
  716.5 116.1 %all-reduce.23.cloned.1.call-start = ((), (), s32[]{:S(2)}) async-start(), calls=%async_computation.5 | async-start | bytes 1048576 | tf_op jit(solution)/shard_map/psum | solution.py:9
Sparse Core Ops, SparseCore 0:
  9.2 26.0 all-gather.8
  37.7 38.6 all-reduce.12
  78.3 23.1 all-gather.10
  114.8 56.5 all-reduce.14
  195.7 48.5 all-reduce.28
  246.0 22.5 all-gather.12
  315.6 55.9 all-reduce.16
  396.0 48.5 all-reduce.26
  446.5 22.5 all-gather.14
  516.3 55.9 all-reduce.18
  596.6 48.5 all-reduce.24
  716.7 55.9 all-reduce.20
  797.4 35.2 all-reduce.22
where the time goes:
time: 883 us; the launch traced here: 874 us
  waiting for transfers between devices  466 us (53%)
  matrix products  305 us (35%)
  blocking collectives  76 us (9%)
  between operations  14 us (2%)
  other arithmetic  11 us (1%)
    psum x4, waiting for transfers between devices, shards(): product_rows = lax.psum(partial_value, 'col')  219 us
    psum x5, waiting for transfers between devices, broadcast(): return lax.psum(kept, axis)  218 us
    dot_general x4, matrix products, shards(): lax.dot_general(reflect_cols, matrix, (((1,), (1,)), ((), ())), precision...  148 us
    dot_general x4, matrix products, shards(): lax.dot_general(left_block, right_block, (((0,), (0,)), ((), ())), precis...  139 us
    psum x4, blocking collectives, shards(): inner = lax.psum(local_inner, 'row')  76 us
    all_gather x4, waiting for transfers between devices, shards(): reflect_rows = lax.all_gather(piece, 'col', axis=1, tiled=True)  26.8 us
  transfers between devices with their start and end apart: 13, of which 10 were waited for; matrix products, arithmetic and copies ran while one was open for 21% of the time, Pallas kernels for 0%

commit v1 on v0

v1 whole, which is shorter than its diff:
```python
import functools

import jax
import jax.numpy as jnp
from jax import lax
from jax.experimental import pallas as pl
from jax.experimental.pallas import tpu as pltpu
from jax.sharding import PartitionSpec as P


F32 = jnp.float32
BF16 = jnp.bfloat16
LANES = 128
VMEM_LIMIT = 60 * 1024 * 1024
NN = ((1,), (0,))
NT = ((1,), (1,))
TN = ((0,), (0,))


def split(value):
    high = value.astype(BF16)
    return high, (value - high.astype(F32)).astype(BF16)


def dot_split(left, right, dims):
    def part(a, b):
        return lax.dot_general(a, b, (dims, ((), ())), preferred_element_type=F32)

    return part(left[0], right[0]) + (part(left[0], right[1]) + part(left[1], right[0]))


def dot_full(a, b, dims=NN):
    return lax.dot_general(
        a, b, (dims, ((), ())), precision=lax.Precision.HIGHEST, preferred_element_type=F32
    )


def params():
    return pltpu.CompilerParams(vmem_limit_bytes=VMEM_LIMIT)


def cost(flops, bytes_accessed):
    return pl.CostEstimate(flops=flops, bytes_accessed=bytes_accessed, transcendentals=0)


def anywhere(count):
    return [pl.BlockSpec(memory_space=pl.ANY)] * count


def exchange(value, offset, count):
    return lax.ppermute(value, "col", [(i, i ^ offset) for i in range(count)])


def ring_shift(value, ring):
    size = len(ring)
    return lax.ppermute(value, "row", [(ring[i], ring[(i + 1) % size]) for i in range(size)])


def fetch(refs, buffer, sems):
    for i, ref in enumerate(refs):
        pltpu.make_async_copy(ref, buffer.at[i], sems.at[i]).start()


def await_fetch(ref, buffer, sems, i):
    pltpu.make_async_copy(ref, buffer.at[i], sems.at[i]).wait()


def columns_kernel(count, pieces, width, table, *refs):
    vs, m_ref, outs, (buffer, sems) = refs[:count], refs[count], refs[count + 1 : -2], refs[-2:]
    step = pl.program_id(0)

    @pl.when(step == 0)
    def _():
        fetch(vs, buffer, sems)

    await_fetch(vs[0], buffer, sems, step)
    left = split(buffer[step])
    for i in range(pieces):
        at = pl.multiple_of(table[1, i] * width, width)
        total = dot_split(left, split(m_ref[:, pl.ds(at, width)]), NN)

        @pl.when(step == 0)
        def _():
            outs[i][...] = total

        @pl.when(step > 0)
        def _():
            outs[i][...] += total


def product_columns(table, vs, matrix, pieces):
    count = len(vs)
    vectors, tile = vs[0].shape
    cols = matrix.shape[1]
    width = cols // pieces
    piece = pl.BlockSpec((vectors, width), lambda s, t: (0, 0))
    return pl.pallas_call(
        functools.partial(columns_kernel, count, pieces, width),
        out_shape=[jax.ShapeDtypeStruct((vectors, width), F32)] * pieces,
        grid_spec=pltpu.PrefetchScalarGridSpec(
            num_scalar_prefetch=1,
            grid=(count,),
            in_specs=anywhere(count) + [pl.BlockSpec((tile, cols), lambda s, t: (t[0, s], 0))],
            out_specs=[piece] * pieces,
            scratch_shapes=[pltpu.VMEM((count, vectors, tile), F32), pltpu.SemaphoreType.DMA((count,))],
        ),
        compiler_params=params(),
        cost_estimate=cost(6 * count * tile * cols * vectors, 4 * count * tile * cols),
        name="product_columns",
    )(table, *vs, matrix)


def rows_kernel(pieces, width, more, table, *refs):
    vcs, refs = refs[:pieces], refs[pieces:]
    m_ref, refs = refs[0], refs[1:]
    before, (out_ref, buffer, high_ref, low_ref, sems) = refs[:more], refs[more:]

    @pl.when(pl.program_id(0) == 0)
    def _():
        fetch(vcs, buffer, sems)
        for k in range(pieces):
            await_fetch(vcs[k], buffer, sems, k)
            high_ref[k], low_ref[k] = split(buffer[k])

    total = before[0][0] if more else None
    for k in range(pieces):
        at = pl.multiple_of(table[2, k] * width, width)
        left = split(m_ref[:, pl.ds(at, width)])
        term = dot_split(left, (high_ref[k], low_ref[k]), NT)
        total = term if total is None else total + term
    out_ref[0] = total


def product_rows(table, first, count, vcs, matrix, before=()):
    pieces = len(vcs)
    vectors, width = vcs[0].shape
    rows, cols = matrix.shape
    tile = rows // (2 * count)
    entry = pl.BlockSpec((1, tile, vectors), lambda s, t: (s, 0, 0))
    return pl.pallas_call(
        functools.partial(rows_kernel, pieces, width, len(before)),
        out_shape=jax.ShapeDtypeStruct((count, tile, vectors), F32),
        grid_spec=pltpu.PrefetchScalarGridSpec(
            num_scalar_prefetch=1,
            grid=(count,),
            in_specs=anywhere(pieces)
            + [pl.BlockSpec((tile, cols), lambda s, t: (t[0, first + s], 0))]
            + [entry] * len(before),
            out_specs=entry,
            scratch_shapes=[pltpu.VMEM((pieces, vectors, width), F32)]
            + [pltpu.VMEM((pieces, vectors, width), BF16)] * 2
            + [pltpu.SemaphoreType.DMA((pieces,))],
        ),
        compiler_params=params(),
        cost_estimate=cost(6 * count * tile * cols * vectors, 4 * count * tile * cols),
        name="product_rows",
    )(table, *vcs, matrix, *before)


def inner_kernel(pieces, nb, table, own_ref, *refs):
    vcs, pcs, out_ref = refs[:pieces], refs[pieces : 2 * pieces], refs[2 * pieces]
    buffer, sems = refs[2 * pieces + 1 :]
    fetch(vcs, buffer, sems)
    own = split(own_ref[...])
    gram = dot_split(own, own, NT)
    for i in range(pieces):
        await_fetch(vcs[i], buffer, sems, i)
    total = None
    for i in range(pieces):
        term = dot_split(split(buffer[table[3, i]]), split(pcs[i][...]), NT)
        total = term if total is None else total + term
    block_row = lax.broadcasted_iota(jnp.int32, gram.shape, 0) // nb
    block_col = lax.broadcasted_iota(jnp.int32, gram.shape, 1) // nb
    out_ref[...] = jnp.where(block_row > block_col, gram, total)


def inner_products(table, own, vcs, pcs, nb):
    pieces = len(vcs)
    vectors, width = vcs[0].shape
    vmem = pl.BlockSpec(memory_space=pltpu.VMEM)
    return pl.pallas_call(
        functools.partial(inner_kernel, pieces, nb),
        out_shape=jax.ShapeDtypeStruct((vectors, vectors), F32),
        in_specs=[pl.BlockSpec(memory_space=pltpu.SMEM), vmem] + anywhere(pieces) + [vmem] * pieces,
        scratch_shapes=[pltpu.VMEM((pieces, vectors, width), F32), pltpu.SemaphoreType.DMA((pieces,))],
        compiler_params=params(),
        cost_estimate=cost(6 * (pieces + 1) * vectors * vectors * width, 8 * pieces * vectors * width),
        name="inner_products",
    )(table, own, *vcs, *pcs)


def coefficients_kernel(panels, blocks_ref, turned_ref, factor_ref, factor_t_ref, a_ref, b_ref, cross_ref):
    a_ref[...] = jnp.zeros_like(a_ref)
    b_ref[...] = jnp.zeros_like(b_ref)
    for p in range(panels):
        inner = turned_ref[p, p]
        for q in range(p):
            total = None
            for i in range(q + 1):
                term = dot_full(turned_ref[p, i], a_ref[q, i], NT) + dot_full(blocks_ref[p, i], b_ref[q, i], NT)
                total = term if total is None else total + term
            cross_ref[q] = total
            inner = inner - (dot_full(blocks_ref[p, q], total, NT) + dot_full(total, blocks_ref[p, q], NT))
        for i in range(p):
            a_sum, b_sum = None, None
            for q in range(i, p):
                term = dot_full(blocks_ref[p, q], a_ref[q, i])
                a_sum = term if a_sum is None else a_sum + term
                term = dot_full(blocks_ref[p, q], b_ref[q, i])
                b_sum = term if b_sum is None else b_sum + term
            a_ref[p, i] = -dot_full(factor_t_ref[p], a_sum)
            b_ref[p, i] = -dot_full(factor_t_ref[p], cross_ref[i] + b_sum)
        a_ref[p, p] = factor_t_ref[p]
        b_ref[p, p] = -0.5 * dot_full(factor_t_ref[p], dot_full(inner, factor_ref[p]))


def coefficients(inner, factor):
    panels, nb, _ = factor.shape
    size = -(-nb // LANES) * LANES
    grown = ((0, size - nb),) * 2
    blocks = inner.reshape(panels, nb, panels, nb).transpose(0, 2, 1, 3)
    blocks = jnp.pad(blocks, ((0, 0), (0, 0)) + grown)
    factor = jnp.pad(factor, ((0, 0),) + grown)
    shape = jax.ShapeDtypeStruct((panels, panels, size, size), F32)
    a, b = pl.pallas_call(
        functools.partial(coefficients_kernel, panels),
        out_shape=[shape, shape],
        in_specs=[pl.BlockSpec(memory_space=pltpu.VMEM)] * 4,
        scratch_shapes=[pltpu.VMEM((panels, size, size), F32)],
        compiler_params=pltpu.CompilerParams(vmem_limit_bytes=VMEM_LIMIT),
        name="coefficients",
    )(blocks, blocks.transpose(1, 0, 3, 2), factor, factor.transpose(0, 2, 1))
    whole = lambda value: value[..., :nb, :nb].transpose(0, 2, 1, 3).reshape(panels * nb, panels * nb)
    return whole(a), whole(b)


def update_kernel(count, pieces, width, table, a_ref, b_ref, m_ref, *refs):
    vcs, pcs, refs = refs[:pieces], refs[pieces : 2 * pieces], refs[2 * pieces :]
    vs, ps, refs = refs[:count], refs[count : 2 * count], refs[2 * count :]
    out_ref, buffer, v_buffer, p_buffer, wh, wl, xh, xl, sems, v_sems, p_sems = refs
    step = pl.program_id(0)

    @pl.when(step == 0)
    def _():
        fetch(vcs + pcs, buffer, sems)
        fetch(vs, v_buffer, v_sems)
        fetch(ps, p_buffer, p_sems)
        a = split(a_ref[...])
        b = split(b_ref[...] + b_ref[...].T)
        for i in range(2 * pieces):
            await_fetch(vcs[0], buffer, sems, i)
        for i in range(pieces):
            cols = pl.ds(pl.multiple_of(table[4, i] * width, width), width)
            v = split(buffer[table[5, i]])
            wh[:, cols], wl[:, cols] = split(dot_split(a, split(buffer[pieces + i]), NN) + dot_split(b, v, NN))
            xh[:, cols], xl[:, cols] = split(dot_split(a, v, TN))

    await_fetch(vs[0], v_buffer, v_sems, step)
    await_fetch(ps[0], p_buffer, p_sems, step)
    half = m_ref.shape[0] // 2
    for part in range(2):
        rows = pl.ds(part * half, half)
        v = split(v_buffer[step, :, rows].T)
        p = split(p_buffer[step, rows, :])
        for i in range(pieces):
            cols = pl.ds(i * width, width)
            term = dot_split(v, (wh[:, cols], wl[:, cols]), NN) + dot_split(p, (xh[:, cols], xl[:, cols]), NN)
            out_ref[rows, cols] = m_ref[rows, cols] - term


def update_matrix(table, a, b, vcs, pcs, vs, ps, matrix):
    pieces, count = len(vcs), len(vs)
    vectors, width = vcs[0].shape
    tile = vs[0].shape[1]
    cols = matrix.shape[1]
    whole = lambda *shape: pl.BlockSpec(shape, lambda s, t: (0,) * len(shape))
    here = pl.BlockSpec((tile, cols), lambda s, t: (t[0, s], 0))
    return pl.pallas_call(
        functools.partial(update_kernel, count, pieces, width),
        out_shape=jax.ShapeDtypeStruct(matrix.shape, F32),
        grid_spec=pltpu.PrefetchScalarGridSpec(
            num_scalar_prefetch=1,
            grid=(count,),
            in_specs=[whole(vectors, vectors), whole(vectors, vectors), here] + anywhere(2 * (pieces + count)),
            out_specs=here,
            scratch_shapes=[
                pltpu.VMEM((2 * pieces, vectors, width), F32),
                pltpu.VMEM((count, vectors, tile), F32),
                pltpu.VMEM((count, tile, vectors), F32),
            ]
            + [pltpu.VMEM((vectors, cols), BF16)] * 4
            + [pltpu.SemaphoreType.DMA((n,)) for n in (2 * pieces, count, count)],
        ),
        compiler_params=params(),
        cost_estimate=cost(12 * count * tile * cols * vectors, 8 * count * tile * cols),
        name="update_matrix",
    )(table, a, b, matrix, *vcs, *pcs, *vs, *ps)


def total_over_all(value, row_count, col_count):
    value = value + exchange(value, 1, col_count)
    parity = lax.axis_index("col") % 2
    height = value.shape[0] // 2
    mine = lax.dynamic_slice_in_dim(value, parity * height, height, 0)
    bit = 2
    while bit < col_count:
        mine = mine + exchange(mine, bit, col_count)
        bit *= 2
    total = mine
    for shift in range(1, row_count):
        total = total + lax.ppermute(mine, "row", [(i, (i + shift) % row_count) for i in range(row_count)])
    other = exchange(total, 1, col_count)
    first = jnp.where(parity == 0, total, other)
    second = jnp.where(parity == 0, other, total)
    return jnp.concatenate([first, second], axis=0)


def shards(symmetric, reflectors, tri_factor):
    row_count = lax.axis_size("row")
    col_count = lax.axis_size("col")
    row = lax.axis_index("row")
    col = lax.axis_index("col")
    panels, nb, own_width = reflectors.shape
    vectors = panels * nb
    per_row = col_count // row_count
    pairs = col_count // 2

    ring = [0] + list(range(1, row_count, 2)) + list(range(2, row_count, 2))[::-1]
    ring_array = jnp.array(ring, jnp.int32)
    place_of = jnp.array([ring.index(i) for i in range(row_count)], jnp.int32)
    place = place_of[row]
    offsets = list(range(0, col_count, 2)) + list(range(1, col_count, 2))
    block = col // per_row
    steps = jnp.arange(row_count, dtype=jnp.int32)

    def padded(entries):
        return jnp.pad(entries, (0, col_count - entries.shape[0]))

    sent = ring_array[(place - 1 - steps) % row_count]
    gathered = ring_array[(place - steps) % row_count]
    table = jnp.stack(
        [
            col ^ jnp.array(offsets, jnp.int32),
            padded(sent),
            padded((block - steps) % row_count),
            padded((block - sent) % row_count),
            padded(gathered),
            padded((block - gathered) % row_count),
        ]
    ).astype(jnp.int32)

    own = reflectors.reshape(vectors, own_width)

    near = [own] + [exchange(own, offset, col_count) for offset in offsets[1:pairs]]
    far = [exchange(piece, 1, col_count) for piece in near]

    around = [own]
    for _ in range(row_count - 1):
        around.append(ring_shift(around[-1], ring))
    around, far = lax.optimization_barrier((around, far))
    vcs = []
    for k in range(row_count):
        target = [(j % row_count + k) % row_count * per_row + j // row_count for j in range(col_count)]
        wanted = (place - place_of[(col % row_count + k) % row_count]) % row_count
        piece = around[0]
        for i in range(1, row_count):
            piece = jnp.where(wanted == i, around[i], piece)
        vcs.append(lax.ppermute(piece, "col", list(enumerate(target))))

    partial = product_columns(table, near + far, symmetric, row_count)
    partial, vcs = lax.optimization_barrier((partial, vcs))

    total = partial[0]
    for i in range(1, row_count):
        total = ring_shift(total, ring) + partial[i]
    pcs = [total]
    for _ in range(row_count - 1):
        pcs.append(ring_shift(pcs[-1], ring))

    other = product_rows(table, pairs, pairs, vcs, symmetric)
    other = exchange(other, 1, col_count)
    mine = product_rows(table, 0, pairs, vcs, symmetric, (other,))

    share = inner_products(table, own, vcs, partial, nb)
    inner = total_over_all(share, row_count, col_count)
    a, b = coefficients(inner, tri_factor)

    total = mine[0]
    for i in range(1, pairs):
        total = total + exchange(mine[i], offsets[i], col_count)
    near_rows = [total] + [exchange(total, offset, col_count) for offset in offsets[1:pairs]]
    far_rows = [exchange(piece, 1, col_count) for piece in near_rows]

    return update_matrix(table, a, b, vcs, pcs, near + far, near_rows + far_rows, symmetric)


def solution(mesh):
    placed = (P("row", "col"), P(None, None, ("row", "col")), P())
    return jax.shard_map(shards, mesh=mesh, in_specs=placed, out_specs=P("row", "col"), check_vma=False)
```

time: 883 us -> 282 us (0.32)
  waiting for transfers between devices: 466 us -> 94.5 us
  matrix products: 305 us -> 0 us
  Pallas kernels: 0 us -> 114 us
  blocking collectives: 76 us -> 0 us
  starting transfers between devices: 0.66 us -> 42.2 us
  local copies, waits for them, and re-layouts: 1.96 us -> 19.2 us
    psum x9 -> x0, waiting for transfers between devices: 437 us -> none  [the longest x4 219 us: shards(): product_rows = lax.psum(partial_value, 'col')]
    dot_general x24 -> x0, matrix products: 305 us -> none  [the longest x4 148 us: shards(): lax.dot_general(reflect_cols, matrix, (((1,), (1,)), ((), ())), precision...]
    pallas_call x0 -> x6, Pallas kernels: none -> 114 us  [the longest x1 41.6 us: update_matrix(): pl.pallas_call(functools.partial(update_kernel, count, pieces, width), ou...]
    ppermute x0 -> x38, waiting for transfers between devices: none -> 94.5 us  [the longest x9 50 us: ring_shift(): lax.ppermute(value, 'row', [(ring[i], ring[(i + 1) % size]) for i in rang...]
    psum x4 -> x0, blocking collectives: 76 us -> none  [shards(): inner = lax.psum(local_inner, 'row')]
    ppermute x0 -> x38, starting transfers between devices: none -> 42.2 us  [the longest x22 18.2 us: exchange(): return lax.ppermute(value, 'col', [(i, i ^ offset) for i in range(count)])]
    all_gather x4 -> x0, waiting for transfers between devices: 26.8 us -> none  [shards(): reflect_rows = lax.all_gather(piece, 'col', axis=1, tiled=True)]
  transfers between devices with their start and end apart: 13 -> 38, of which waited for: 10 -> 12; matrix products, arithmetic and copies ran while one was open for 21% -> 7% of each run, Pallas kernels for 0% -> 21%
where the time goes in v1:
time: 282 us; the launch traced here: 281 us
  Pallas kernels  114 us (40%)
  waiting for transfers between devices  94.5 us (34%)
  starting transfers between devices  42.2 us (15%)
  local copies, waits for them, and re-layouts  19.2 us (7%)
  between operations  6.36 us (2%)
  other arithmetic  5.23 us (2%)
    ppermute x9, waiting for transfers between devices, ring_shift(): lax.ppermute(value, 'row', [(ring[i], ring[(i + 1) % size]) for i in rang...  50 us
    pallas_call x1, Pallas kernels, update_matrix(): pl.pallas_call(functools.partial(update_kernel, count, pieces, width), ou...  41.6 us
    ppermute x22, waiting for transfers between devices, exchange(): return lax.ppermute(value, 'col', [(i, i ^ offset) for i in range(count)])  41 us
    pallas_call x2, Pallas kernels, product_rows(): pl.pallas_call(functools.partial(rows_kernel, pieces, width, len(before))...  28.2 us
    pallas_call x1, Pallas kernels, product_columns(): pl.pallas_call(functools.partial(columns_kernel, count, pieces, width), o...  26.3 us
    ppermute x22, starting transfers between devices, exchange(): return lax.ppermute(value, 'col', [(i, i ^ offset) for i in range(count)])  18.2 us
    pallas_call x1, Pallas kernels, coefficients(): pl.pallas_call(functools.partial(coefficients_kernel, panels), out_shape=...  12.4 us
    ppermute x9, starting transfers between devices, ring_shift(): lax.ppermute(value, 'row', [(ring[i], ring[(i + 1) % size]) for i in rang...  11.1 us
  transfers between devices with their start and end apart: 38, of which 12 were waited for; matrix products, arithmetic and copies ran while one was open for 7% of the time, Pallas kernels for 21%

profile of v1, /device:TPU:0, one launch (start us, length us, event | category | flops | bytes accessed | tf_op | source)
XLA Modules:
  0.0 281.3 jit_solution(10455404035662642945)
XLA Ops:
  0.0 3.1 %collective-permute-start.3 = (f32[256,512]{1,0:T(8,128)}, f32[256,512]{1,0:T(8,128)S(1)}, u32[]{:S(2)}, u32[]{:S(2)}) collective-permute-start(f32[256,512]{1,0:T(8,128)} %bitcast.47), channel_id=1, source_target_pairs={{0,8},{8,24},{24,16},{16,0},{1,9},{9,25},{25,17},{17,1},{2,10},{10... | collective-permute-start | bytes 1572872 | tf_op jit(solution)/shard_map/ppermute | solution.py:56
  3.1 2.4 collective-permute-start.2
  6.5 1.5 fusion.10
  19.7 10.0 %collective-permute-done.1.refs_2_.refs_10_ = f32[256,512]{1,0:T(8,128)S(1)} collective-permute-done((f32[256,512]{1,0:T(8,128)}, f32[256,512]{1,0:T(8,128)S(1)}, u32[]{:S(2)}, u32[]{:S(2)}) %collective-permute-start.1) | collective-permute-done | bytes 524320 | tf_op jit(solution)/shard_map/ppermute | solution.py:51
  30.3 2.6 collective-permute-start.5
  34.9 10.2 %collective-permute-done.5 = f32[256,512]{1,0:T(8,128)S(1)} collective-permute-done((f32[256,512]{1,0:T(8,128)S(1)}, f32[256,512]{1,0:T(8,128)S(1)}, u32[]{:S(2)}, u32[]{:S(2)}) %collective-permute-start.5) | collective-permute-done | bytes 524320 | tf_op jit(solution)/shard_map/ppermute | solution.py:56
  45.2 2.2 select_select_fusion
  47.4 3.5 %collective-permute-start.13 = (f32[256,512]{1,0:T(8,128)}, f32[256,512]{1,0:T(8,128)S(1)}, u32[]{:S(2)}, u32[]{:S(2)}) collective-permute-start(f32[256,512]{1,0:T(8,128)} %get-tuple-element.52), channel_id=1, source_target_pairs={{0,6},{1,0},{2,2},{3,4},{4,7},{5,1},{6,3},{7,5},{8,14},{9,8},{10,1... | collective-permute-start | bytes 1572872 | tf_op jit(solution)/shard_map/ppermute | solution.py:368
  51.0 3.9 %collective-permute-start.11 = (f32[256,512]{1,0:T(8,128)S(1)}, f32[256,512]{1,0:T(8,128)S(1)}, u32[]{:S(2)}, u32[]{:S(2)}) collective-permute-start(f32[256,512]{1,0:T(8,128)S(1)} %get-tuple-element.54), channel_id=1, source_target_pairs={{0,2},{1,4},{2,6},{3,0},{4,3},{5,5},{6,7},{7,1},{8,10},{9,12},{10,... | collective-permute-start | bytes 1572872 | tf_op jit(solution)/shard_map/ppermute | solution.py:368
  55.6 26.3 %product_columns.1 = (f32[256,512]{1,0:T(8,128)}, f32[256,512]{1,0:T(8,128)}, f32[256,512]{1,0:T(8,128)}, f32[256,512]{1,0:T(8,128)}) custom-call(s32[6,8]{1,0:T(8,128)} %stack.27.table, f32[256,512]{1,0:T(8,128)} %bitcast.53, f32[256,512]{1,0:T(8,128)} %collective-permute-done.refs_1_.refs_9_, f32[256,512]{1,0:T(8,128)} %copy-done.16, ...), custom_call_target="tpu_custom_call" | custom-call | flops 12884901888 | bytes 33554432 | tf_op jit(solution)/shard_map/product_columns/pallas_call | solution.py:97
  83.3 14.0 %product_rows.2 = f32[4,512,256]{2,1,0:T(8,128)} custom-call(s32[6,8]{1,0:T(8,128)} %stack.27.table, f32[256,512]{1,0:T(8,128)} %copy-done.3, f32[256,512]{1,0:T(8,128)} %copy-done.2, f32[256,512]{1,0:T(8,128)} %copy-done.1, f32[256,512]{1,0:T(8,128)} %copy-done, f32[4096,2048]{1,0:T(8,128)} %m_ref.1), custom_call_target="tpu_custom_call" | custom-call | flops 6442450944 | bytes 16777216 | tf_op jit(solution)/shard_map/product_rows/pallas_call | solution.py:140
  98.7 1.7 collective-permute-start.21
  100.4 13.1 %collective-permute-done.21 = f32[256,512]{1,0:T(8,128)S(1)} collective-permute-done((f32[256,512]{1,0:T(8,128)S(1)}, f32[256,512]{1,0:T(8,128)S(1)}, u32[]{:S(2)}, u32[]{:S(2)}) %collective-permute-start.21) | collective-permute-done | bytes 524320 | tf_op jit(solution)/shard_map/ppermute | solution.py:56
  114.4 13.2 %collective-permute-done.22 = f32[256,512]{1,0:T(8,128)S(1)} collective-permute-done((f32[256,512]{1,0:T(8,128)S(1)}, f32[256,512]{1,0:T(8,128)S(1)}, u32[]{:S(2)}, u32[]{:S(2)}) %collective-permute-start.22) | collective-permute-done | bytes 524320 | tf_op jit(solution)/shard_map/ppermute | solution.py:56
  127.8 5.2 %inner_products.1 = f32[256,256]{1,0:T(8,128)} custom-call(s32[6,8]{1,0:T(8,128)} %stack.27.table, f32[256,512]{1,0:T(8,128)} %bitcast.54, f32[256,512]{1,0:T(8,128)} %copy-done.3, f32[256,512]{1,0:T(8,128)} %copy-done.2, f32[256,512]{1,0:T(8,128)} %copy-done.1, f32[256,512]{1,0:T(8,128)} %copy-done, f32[256,512]{1,0:T(8,128)} %get-tuple-element.43.refs_4_, ...), custom_call_target="tpu_custom_call" | custom-call | flops 1006632960 | bytes 4194304 | tf_op jit(solution)/shard_map/inner_products/pallas_call | solution.py:181
  133.1 7.8 %collective-permute-done.23 = f32[256,512]{1,0:T(8,128)S(1)} collective-permute-done((f32[256,512]{1,0:T(8,128)S(1)}, f32[256,512]{1,0:T(8,128)S(1)}, u32[]{:S(2)}, u32[]{:S(2)}) %collective-permute-start.23) | collective-permute-done | bytes 524320 | tf_op jit(solution)/shard_map/ppermute | solution.py:56
  142.4 14.2 %product_rows.3 = f32[4,512,256]{2,1,0:T(8,128)} custom-call(s32[6,8]{1,0:T(8,128)} %stack.27.table, f32[256,512]{1,0:T(8,128)} %copy-done.3, f32[256,512]{1,0:T(8,128)} %copy-done.2, f32[256,512]{1,0:T(8,128)} %copy-done.1, f32[256,512]{1,0:T(8,128)} %copy-done, f32[4096,2048]{1,0:T(8,128)} %m_ref.1, f32[4,512,256]{2,1,0:T(8,128)} %copy-done.4), custom_call_target="tpu_custom_call" | custom-call | flops 6442450944 | bytes 16777216 | tf_op jit(solution)/shard_map/product_rows/pallas_call | solution.py:140
  156.7 2.5 slice_bitcast_fusion.2
  159.1 2.9 %collective-permute-start.28 = (f32[512,256]{1,0:T(8,128)}, f32[512,256]{1,0:T(8,128)S(1)}, u32[]{:S(2)}, u32[]{:S(2)}) collective-permute-start(f32[512,256]{1,0:T(8,128)} %get-tuple-element.49), channel_id=1, source_target_pairs={{0,2},{1,3},{2,0},{3,1},{4,6},{5,7},{6,4},{7,5},{8,10},{9,11},{10,... | collective-permute-start | bytes 1572872 | tf_op jit(solution)/shard_map/ppermute | solution.py:51
  162.0 1.5 collective-permute-start.29
  163.6 2.1 collective-permute-start.15
  165.6 20.7 %collective-permute-done.15 = f32[128,256]{1,0:T(8,128)S(1)} collective-permute-done((f32[128,256]{1,0:T(8,128)S(1)}, f32[128,256]{1,0:T(8,128)S(1)}, u32[]{:S(2)}, u32[]{:S(2)}) %collective-permute-start.15) | collective-permute-done | bytes 131104 | tf_op jit(solution)/shard_map/ppermute | solution.py:51
  186.4 5.0 %collective-permute-done.16 = f32[128,256]{1,0:T(8,128)S(1)} collective-permute-done((f32[128,256]{1,0:T(8,128)S(1)}, f32[128,256]{1,0:T(8,128)S(1)}, u32[]{:S(2)}, u32[]{:S(2)}) %collective-permute-start.16) | collective-permute-done | bytes 131104 | tf_op jit(solution)/shard_map/ppermute | solution.py:51
  191.4 2.5 collective-permute-start.19
  193.9 1.6 collective-permute-start.18
  200.0 2.0 collective-permute-start.32
  202.0 3.5 %collective-permute-done.18 = f32[128,256]{1,0:T(8,128)S(1)} collective-permute-done((f32[128,256]{1,0:T(8,128)S(1)}, f32[128,256]{1,0:T(8,128)S(1)}, u32[]{:S(2)}, u32[]{:S(2)}) %collective-permute-start.18) | collective-permute-done | bytes 131104 | tf_op jit(solution)/shard_map/ppermute | solution.py:311
  205.5 1.7 collective-permute-start.31
  210.1 4.5 %collective-permute-done.25.refs_6_ = f32[256,512]{1,0:T(8,128)} collective-permute-done((f32[256,512]{1,0:T(8,128)}, f32[256,512]{1,0:T(8,128)}, u32[]{:S(2)}, u32[]{:S(2)}) %collective-permute-start.25) | collective-permute-done | bytes 524320 | tf_op jit(solution)/shard_map/ppermute | solution.py:56
  214.8 5.3 %collective-permute-done.32.refs_18_ = f32[512,256]{1,0:T(8,128)} collective-permute-done((f32[512,256]{1,0:T(8,128)S(1)}, f32[512,256]{1,0:T(8,128)}, u32[]{:S(2)}, u32[]{:S(2)}) %collective-permute-start.32) | collective-permute-done | bytes 524320 | tf_op jit(solution)/shard_map/ppermute | solution.py:51
  222.9 12.4 %coefficients.1 = (f32[4,4,128,128]{3,2,1,0:T(8,128)}, f32[4,4,128,128]{3,2,1,0:T(8,128)}) custom-call(f32[4,4,128,128]{3,2,1,0:T(8,128)} %pad.29.clone.blocks_ref, f32[4,4,128,128]{3,2,1,0:T(8,128)} %pad_bitcast_fusion.turned_ref, f32[4,128,128]{2,1,0:T(8,128)} %pad.30.clone.factor_ref, f32[4,128,128]{2,1,0:T(8,128)} %pad_bitcast_fusion.1.factor_t_ref), custom_call_target="tpu_custom_call" | custom-call | tf_op jit(solution)/shard_map/coefficients/pallas_call | solution.py:225
  239.5 41.6 %update_matrix.1 = f32[4096,2048]{1,0:T(8,128)} custom-call(s32[6,8]{1,0:T(8,128)} %stack.27.table, f32[256,256]{1,0:T(8,128)} %reshape.112.a_ref, f32[256,256]{1,0:T(8,128)} %reshape.113.b_ref, f32[4096,2048]{1,0:T(8,128)} %m_ref.1, f32[256,512]{1,0:T(8,128)} %copy-done.3, f32[256,512]{1,0:T(8,128)} %copy-done.2, f32[256,512]{1,0:T(8,128)} %copy-done.1, ...), custom_call_target="tpu_custom_call" | custom-call | flops 25769803776 | bytes 67108864 | tf_op jit(solution)/shard_map/update_matrix/pallas_call | solution.py:278
  (127 shorter events, 30.2 us)
Async XLA Ops:
  0.0 16.2 %collective-permute-start.3 = (f32[256,512]{1,0:T(8,128)}, f32[256,512]{1,0:T(8,128)S(1)}, u32[]{:S(2)}, u32[]{:S(2)}) collective-permute-start(f32[256,512]{1,0:T(8,128)} %bitcast.47), channel_id=1, source_target_pairs={{0,8},{8,24},{24,16},{16,0},{1,9},{9,25},{25,17},{17,1},{2,10},{10... | collective-permute-start | bytes 1572872 | tf_op jit(solution)/shard_map/ppermute | solution.py:56
  3.1 31.1 %collective-permute-start.6 = (f32[256,512]{1,0:T(8,128)}, f32[256,512]{1,0:T(8,128)S(1)}, u32[]{:S(2)}, u32[]{:S(2)}) collective-permute-start(f32[256,512]{1,0:T(8,128)} %bitcast.48), channel_id=1, source_target_pairs={{0,1},{1,0},{2,3},{3,2},{4,5},{5,4},{6,7},{7,6},{8,9},{9,8},{10,11... | collective-permute-start | bytes 1572872 | tf_op jit(solution)/shard_map/ppermute | solution.py:51
  3.1 16.6 %collective-permute-start.2 = (f32[256,512]{1,0:T(8,128)}, f32[256,512]{1,0:T(8,128)S(1)}, u32[]{:S(2)}, u32[]{:S(2)}) collective-permute-start(f32[256,512]{1,0:T(8,128)} %bitcast.49), channel_id=1, source_target_pairs={{0,6},{1,7},{2,4},{3,5},{4,2},{5,3},{6,0},{7,1},{8,14},{9,15},{10,... | collective-permute-start | bytes 1572872 | tf_op jit(solution)/shard_map/ppermute | solution.py:51
  5.5 24.2 %collective-permute-start.1 = (f32[256,512]{1,0:T(8,128)}, f32[256,512]{1,0:T(8,128)S(1)}, u32[]{:S(2)}, u32[]{:S(2)}) collective-permute-start(f32[256,512]{1,0:T(8,128)} %bitcast.50), channel_id=1, source_target_pairs={{0,4},{1,5},{2,6},{3,7},{4,0},{5,1},{6,2},{7,3},{8,12},{9,13},{10,... | collective-permute-start | bytes 1572872 | tf_op jit(solution)/shard_map/ppermute | solution.py:51
  6.0 23.9 %collective-permute-start = (f32[256,512]{1,0:T(8,128)}, f32[256,512]{1,0:T(8,128)}, u32[]{:S(2)}, u32[]{:S(2)}) collective-permute-start(f32[256,512]{1,0:T(8,128)} %bitcast.51), channel_id=1, source_target_pairs={{0,2},{1,3},{2,0},{3,1},{4,6},{5,7},{6,4},{7,5},{8,10},{9,11},{10,... | collective-permute-start | bytes 1572872 | tf_op jit(solution)/shard_map/ppermute | solution.py:51
  16.2 14.1 %collective-permute-start.4 = (f32[256,512]{1,0:T(8,128)S(1)}, f32[256,512]{1,0:T(8,128)S(1)}, u32[]{:S(2)}, u32[]{:S(2)}) collective-permute-start(f32[256,512]{1,0:T(8,128)S(1)} %collective-permute-done.3), channel_id=1, source_target_pairs={{0,8},{8,24},{24,16},{16,0},{1,9},{9,25},{25,17},{17,1},{2,10},{10... | collective-permute-start | bytes 1572872 | tf_op jit(solution)/shard_map/ppermute | solution.py:56
  19.6 14.5 %collective-permute-start.9 = (f32[256,512]{1,0:T(8,128)S(1)}, f32[256,512]{1,0:T(8,128)}, u32[]{:S(2)}, u32[]{:S(2)}) collective-permute-start(f32[256,512]{1,0:T(8,128)S(1)} %collective-permute-done.2.refs_3_.refs_11_), channel_id=1, source_target_pairs={{0,1},{1,0},{2,3},{3,2},{4,5},{5,4},{6,7},{7,6},{8,9},{9,8},{10,11... | collective-permute-start | bytes 1572872 | tf_op jit(solution)/shard_map/ppermute | solution.py:51
  30.3 14.9 %collective-permute-start.5 = (f32[256,512]{1,0:T(8,128)S(1)}, f32[256,512]{1,0:T(8,128)S(1)}, u32[]{:S(2)}, u32[]{:S(2)}) collective-permute-start(f32[256,512]{1,0:T(8,128)S(1)} %collective-permute-done.4), channel_id=1, source_target_pairs={{0,8},{8,24},{24,16},{16,0},{1,9},{9,25},{25,17},{17,1},{2,10},{10... | collective-permute-start | bytes 1572872 | tf_op jit(solution)/shard_map/ppermute | solution.py:56
  47.4 34.6 %collective-permute-start.13 = (f32[256,512]{1,0:T(8,128)}, f32[256,512]{1,0:T(8,128)S(1)}, u32[]{:S(2)}, u32[]{:S(2)}) collective-permute-start(f32[256,512]{1,0:T(8,128)} %get-tuple-element.52), channel_id=1, source_target_pairs={{0,6},{1,0},{2,2},{3,4},{4,7},{5,1},{6,3},{7,5},{8,14},{9,8},{10,1... | collective-permute-start | bytes 1572872 | tf_op jit(solution)/shard_map/ppermute | solution.py:368
  50.9 31.1 %collective-permute-start.12 = (f32[256,512]{1,0:T(8,128)S(1)}, f32[256,512]{1,0:T(8,128)S(1)}, u32[]{:S(2)}, u32[]{:S(2)}) collective-permute-start(f32[256,512]{1,0:T(8,128)S(1)} %get-tuple-element.53), channel_id=1, source_target_pairs={{0,4},{1,6},{2,0},{3,2},{4,5},{5,7},{6,1},{7,3},{8,12},{9,14},{10,... | collective-permute-start | bytes 1572872 | tf_op jit(solution)/shard_map/ppermute | solution.py:368
  51.0 31.0 %collective-permute-start.11 = (f32[256,512]{1,0:T(8,128)S(1)}, f32[256,512]{1,0:T(8,128)S(1)}, u32[]{:S(2)}, u32[]{:S(2)}) collective-permute-start(f32[256,512]{1,0:T(8,128)S(1)} %get-tuple-element.54), channel_id=1, source_target_pairs={{0,2},{1,4},{2,6},{3,0},{4,3},{5,5},{6,7},{7,1},{8,10},{9,12},{10,... | collective-permute-start | bytes 1572872 | tf_op jit(solution)/shard_map/ppermute | solution.py:368
  54.9 27.1 %collective-permute-start.10 = (f32[256,512]{1,0:T(8,128)S(1)}, f32[256,512]{1,0:T(8,128)S(1)}, u32[]{:S(2)}, u32[]{:S(2)}) collective-permute-start(f32[256,512]{1,0:T(8,128)S(1)} %get-tuple-element.55), channel_id=1, source_target_pairs={{0,0},{1,2},{2,4},{3,6},{4,1},{5,3},{6,5},{7,7},{8,8},{9,10},{10,1... | collective-permute-start | bytes 1572872 | tf_op jit(solution)/shard_map/ppermute | solution.py:368
  97.3 43.7 %collective-permute-start.27 = (f32[4,512,256]{2,1,0:T(8,128)}, f32[4,512,256]{2,1,0:T(8,128)S(1)}, u32[]{:S(2)}, u32[]{:S(2)}) collective-permute-start(f32[4,512,256]{2,1,0:T(8,128)} %product_rows.2), channel_id=1, source_target_pairs={{0,1},{1,0},{2,3},{3,2},{4,5},{5,4},{6,7},{7,6},{8,9},{9,8},{10,11... | collective-permute-start | bytes 6291464 | tf_op jit(solution)/shard_map/ppermute | solution.py:51
  98.7 14.8 %collective-permute-start.21 = (f32[256,512]{1,0:T(8,128)S(1)}, f32[256,512]{1,0:T(8,128)S(1)}, u32[]{:S(2)}, u32[]{:S(2)}) collective-permute-start(f32[256,512]{1,0:T(8,128)S(1)} %copy-done.11), channel_id=1, source_target_pairs={{0,8},{8,24},{24,16},{16,0},{1,9},{9,25},{25,17},{17,1},{2,10},{10... | collective-permute-start | bytes 1572872 | tf_op jit(solution)/shard_map/ppermute | solution.py:56
  113.6 14.0 %collective-permute-start.22 = (f32[256,512]{1,0:T(8,128)S(1)}, f32[256,512]{1,0:T(8,128)S(1)}, u32[]{:S(2)}, u32[]{:S(2)}) collective-permute-start(f32[256,512]{1,0:T(8,128)S(1)} %add.201), channel_id=1, source_target_pairs={{0,8},{8,24},{24,16},{16,0},{1,9},{9,25},{25,17},{17,1},{2,10},{10... | collective-permute-start | bytes 1572872 | tf_op jit(solution)/shard_map/ppermute | solution.py:56
  127.7 13.1 %collective-permute-start.23 = (f32[256,512]{1,0:T(8,128)S(1)}, f32[256,512]{1,0:T(8,128)S(1)}, u32[]{:S(2)}, u32[]{:S(2)}) collective-permute-start(f32[256,512]{1,0:T(8,128)S(1)} %add.202), channel_id=1, source_target_pairs={{0,8},{8,24},{24,16},{16,0},{1,9},{9,25},{25,17},{17,1},{2,10},{10... | collective-permute-start | bytes 1572872 | tf_op jit(solution)/shard_map/ppermute | solution.py:56
  133.0 30.5 %collective-permute-start.14 = (f32[256,256]{1,0:T(8,128)}, f32[256,256]{1,0:T(8,128)S(1)}, u32[]{:S(2)}, u32[]{:S(2)}) collective-permute-start(f32[256,256]{1,0:T(8,128)} %inner_products.1), channel_id=1, source_target_pairs={{0,1},{1,0},{2,3},{3,2},{4,5},{5,4},{6,7},{7,6},{8,9},{9,8},{10,11... | collective-permute-start | bytes 786440 | tf_op jit(solution)/shard_map/ppermute | solution.py:51
  140.9 53.0 %collective-permute-start.24 = (f32[256,512]{1,0:T(8,128)S(1)}, f32[256,512]{1,0:T(8,128)}, u32[]{:S(2)}, u32[]{:S(2)}) collective-permute-start(f32[256,512]{1,0:T(8,128)S(1)} %add.203.refs_4_), channel_id=1, source_target_pairs={{0,8},{8,24},{24,16},{16,0},{1,9},{9,25},{25,17},{17,1},{2,10},{10... | collective-permute-start | bytes 1572872 | tf_op jit(solution)/shard_map/ppermute | solution.py:56
  159.1 36.4 %collective-permute-start.28 = (f32[512,256]{1,0:T(8,128)}, f32[512,256]{1,0:T(8,128)S(1)}, u32[]{:S(2)}, u32[]{:S(2)}) collective-permute-start(f32[512,256]{1,0:T(8,128)} %get-tuple-element.49), channel_id=1, source_target_pairs={{0,2},{1,3},{2,0},{3,1},{4,6},{5,7},{6,4},{7,5},{8,10},{9,11},{10,... | collective-permute-start | bytes 1572872 | tf_op jit(solution)/shard_map/ppermute | solution.py:51
  162.0 34.0 %collective-permute-start.30 = (f32[512,256]{1,0:T(8,128)}, f32[512,256]{1,0:T(8,128)S(1)}, u32[]{:S(2)}, u32[]{:S(2)}) collective-permute-start(f32[512,256]{1,0:T(8,128)} %get-tuple-element.50), channel_id=1, source_target_pairs={{0,6},{1,7},{2,4},{3,5},{4,2},{5,3},{6,0},{7,1},{8,14},{9,15},{10,... | collective-permute-start | bytes 1572872 | tf_op jit(solution)/shard_map/ppermute | solution.py:51
  162.0 35.4 %collective-permute-start.29 = (f32[512,256]{1,0:T(8,128)S(1)}, f32[512,256]{1,0:T(8,128)}, u32[]{:S(2)}, u32[]{:S(2)}) collective-permute-start(f32[512,256]{1,0:T(8,128)S(1)} %get-tuple-element.51), channel_id=1, source_target_pairs={{0,4},{1,5},{2,6},{3,7},{4,0},{5,1},{6,2},{7,3},{8,12},{9,13},{10,... | collective-permute-start | bytes 1572872 | tf_op jit(solution)/shard_map/ppermute | solution.py:51
  163.6 22.7 %collective-permute-start.15 = (f32[128,256]{1,0:T(8,128)S(1)}, f32[128,256]{1,0:T(8,128)S(1)}, u32[]{:S(2)}, u32[]{:S(2)}) collective-permute-start(f32[128,256]{1,0:T(8,128)S(1)} %dynamic-slice_add_fusion), channel_id=1, source_target_pairs={{0,2},{1,3},{2,0},{3,1},{4,6},{5,7},{6,4},{7,5},{8,10},{9,11},{10,... | collective-permute-start | bytes 393224 | tf_op jit(solution)/shard_map/ppermute | solution.py:51
  195.6 11.7 %collective-permute-start.17 = (f32[128,256]{1,0:T(8,128)S(1)}, f32[128,256]{1,0:T(8,128)S(1)}, u32[]{:S(2)}, u32[]{:S(2)}) collective-permute-start(f32[128,256]{1,0:T(8,128)S(1)} %add.197), channel_id=1, source_target_pairs={{0,8},{8,16},{16,24},{24,0},{1,9},{9,17},{17,25},{25,1},{2,10},{10... | collective-permute-start | bytes 393224 | tf_op jit(solution)/shard_map/ppermute | solution.py:311
  196.0 18.7 %collective-permute-start.25 = (f32[256,512]{1,0:T(8,128)}, f32[256,512]{1,0:T(8,128)}, u32[]{:S(2)}, u32[]{:S(2)}) collective-permute-start(f32[256,512]{1,0:T(8,128)} %collective-permute-done.24.refs_5_), channel_id=1, source_target_pairs={{0,8},{8,24},{24,16},{16,0},{1,9},{9,25},{25,17},{17,1},{2,10},{10... | collective-permute-start | bytes 1572872 | tf_op jit(solution)/shard_map/ppermute | solution.py:56
  198.8 15.9 %collective-permute-start.33 = (f32[512,256]{1,0:T(8,128)S(1)}, f32[512,256]{1,0:T(8,128)S(1)}, u32[]{:S(2)}, u32[]{:S(2)}) collective-permute-start(f32[512,256]{1,0:T(8,128)S(1)} %fusion.2.refs_16_), channel_id=1, source_target_pairs={{0,6},{1,7},{2,4},{3,5},{4,2},{5,3},{6,0},{7,1},{8,14},{9,15},{10,... | collective-permute-start | bytes 1572872 | tf_op jit(solution)/shard_map/ppermute | solution.py:51
  200.0 20.0 %collective-permute-start.32 = (f32[512,256]{1,0:T(8,128)S(1)}, f32[512,256]{1,0:T(8,128)}, u32[]{:S(2)}, u32[]{:S(2)}) collective-permute-start(f32[512,256]{1,0:T(8,128)S(1)} %fusion.2.refs_16_), channel_id=1, source_target_pairs={{0,4},{1,5},{2,6},{3,7},{4,0},{5,1},{6,2},{7,3},{8,12},{9,13},{10,... | collective-permute-start | bytes 1572872 | tf_op jit(solution)/shard_map/ppermute | solution.py:51
  205.5 14.5 %collective-permute-start.31 = (f32[512,256]{1,0:T(8,128)S(1)}, f32[512,256]{1,0:T(8,128)}, u32[]{:S(2)}, u32[]{:S(2)}) collective-permute-start(f32[512,256]{1,0:T(8,128)S(1)} %fusion.2.refs_16_), channel_id=1, source_target_pairs={{0,2},{1,3},{2,0},{3,1},{4,6},{5,7},{6,4},{7,5},{8,10},{9,11},{10,... | collective-permute-start | bytes 1572872 | tf_op jit(solution)/shard_map/ppermute | solution.py:51
  209.6 29.8 %collective-permute-start.34 = (f32[512,256]{1,0:T(8,128)S(1)}, f32[512,256]{1,0:T(8,128)}, u32[]{:S(2)}, u32[]{:S(2)}) collective-permute-start(f32[512,256]{1,0:T(8,128)S(1)} %fusion.2.refs_16_), channel_id=1, source_target_pairs={{0,1},{1,0},{2,3},{3,2},{4,5},{5,4},{6,7},{7,6},{8,9},{9,8},{10,11... | collective-permute-start | bytes 1572872 | tf_op jit(solution)/shard_map/ppermute | solution.py:51
  214.7 24.8 %collective-permute-start.26 = (f32[256,512]{1,0:T(8,128)}, f32[256,512]{1,0:T(8,128)}, u32[]{:S(2)}, u32[]{:S(2)}) collective-permute-start(f32[256,512]{1,0:T(8,128)} %collective-permute-done.25.refs_6_), channel_id=1, source_target_pairs={{0,8},{8,24},{24,16},{16,0},{1,9},{9,25},{25,17},{17,1},{2,10},{10... | collective-permute-start | bytes 1572872 | tf_op jit(solution)/shard_map/ppermute | solution.py:56
  214.7 24.8 %collective-permute-start.37 = (f32[512,256]{1,0:T(8,128)S(1)}, f32[512,256]{1,0:T(8,128)}, u32[]{:S(2)}, u32[]{:S(2)}) collective-permute-start(f32[512,256]{1,0:T(8,128)S(1)} %collective-permute-done.33.refs_19_), channel_id=1, source_target_pairs={{0,1},{1,0},{2,3},{3,2},{4,5},{5,4},{6,7},{7,6},{8,9},{9,8},{10,11... | collective-permute-start | bytes 1572872 | tf_op jit(solution)/shard_map/ppermute | solution.py:51
  220.0 19.4 %collective-permute-start.36 = (f32[512,256]{1,0:T(8,128)}, f32[512,256]{1,0:T(8,128)}, u32[]{:S(2)}, u32[]{:S(2)}) collective-permute-start(f32[512,256]{1,0:T(8,128)} %collective-permute-done.32.refs_18_), channel_id=1, source_target_pairs={{0,1},{1,0},{2,3},{3,2},{4,5},{5,4},{6,7},{7,6},{8,9},{9,8},{10,11... | collective-permute-start | bytes 1572872 | tf_op jit(solution)/shard_map/ppermute | solution.py:51
  220.0 19.4 %collective-permute-start.35 = (f32[512,256]{1,0:T(8,128)}, f32[512,256]{1,0:T(8,128)}, u32[]{:S(2)}, u32[]{:S(2)}) collective-permute-start(f32[512,256]{1,0:T(8,128)} %collective-permute-done.31.refs_17_), channel_id=1, source_target_pairs={{0,1},{1,0},{2,3},{3,2},{4,5},{5,4},{6,7},{7,6},{8,9},{9,8},{10,11... | collective-permute-start | bytes 1572872 | tf_op jit(solution)/shard_map/ppermute | solution.py:51
  (24 other events, 252.3 us)

commit v2 on v1

--- a/solution.py
+++ b/solution.py
@@ -10,7 +10,6 @@
 
 F32 = jnp.float32
 BF16 = jnp.bfloat16
-LANES = 128
 VMEM_LIMIT = 60 * 1024 * 1024
 NN = ((1,), (0,))
 NT = ((1,), (1,))
@@ -29,12 +28,6 @@
     return part(left[0], right[0]) + (part(left[0], right[1]) + part(left[1], right[0]))
 
 
-def dot_full(a, b, dims=NN):
-    return lax.dot_general(
-        a, b, (dims, ((), ())), precision=lax.Precision.HIGHEST, preferred_element_type=F32
-    )
-
-
 def params():
     return pltpu.CompilerParams(vmem_limit_bytes=VMEM_LIMIT)
 
@@ -65,8 +58,9 @@
     pltpu.make_async_copy(ref, buffer.at[i], sems.at[i]).wait()
 
 
-def columns_kernel(count, pieces, width, table, *refs):
-    vs, m_ref, outs, (buffer, sems) = refs[:count], refs[count], refs[count + 1 : -2], refs[-2:]
+def columns_kernel(count, pieces, width, more, table, *refs):
+    vs, m_ref, refs = refs[:count], refs[count], refs[count + 1 :]
+    before, outs, (buffer, sems) = refs[:more], refs[more : more + pieces], refs[-2:]
     step = pl.program_id(0)
 
     @pl.when(step == 0)
@@ -81,33 +75,35 @@
 
         @pl.when(step == 0)
         def _():
-            outs[i][...] = total
+            outs[i][...] = total + before[i][...] if more else total
 
         @pl.when(step > 0)
         def _():
             outs[i][...] += total
 
 
-def product_columns(table, vs, matrix, pieces):
+def product_columns(table, first, vs, matrix, pieces, before=()):
     count = len(vs)
     vectors, tile = vs[0].shape
     cols = matrix.shape[1]
     width = cols // pieces
     piece = pl.BlockSpec((vectors, width), lambda s, t: (0, 0))
     return pl.pallas_call(
-        functools.partial(columns_kernel, count, pieces, width),
+        functools.partial(columns_kernel, count, pieces, width, len(before)),
         out_shape=[jax.ShapeDtypeStruct((vectors, width), F32)] * pieces,
         grid_spec=pltpu.PrefetchScalarGridSpec(
             num_scalar_prefetch=1,
             grid=(count,),
-            in_specs=anywhere(count) + [pl.BlockSpec((tile, cols), lambda s, t: (t[0, s], 0))],
+            in_specs=anywhere(count)
+            + [pl.BlockSpec((tile, cols), lambda s, t: (t[0, first + s], 0))]
+            + [piece] * len(before),
             out_specs=[piece] * pieces,
             scratch_shapes=[pltpu.VMEM((count, vectors, tile), F32), pltpu.SemaphoreType.DMA((count,))],
         ),
         compiler_params=params(),
         cost_estimate=cost(6 * count * tile * cols * vectors, 4 * count * tile * cols),
         name="product_columns",
-    )(table, *vs, matrix)
+    )(table, *vs, matrix, *before)
 
 
 def rows_kernel(pieces, width, more, table, *refs):
@@ -189,49 +185,62 @@
     )(table, own, *vcs, *pcs)
 
 
-def coefficients_kernel(panels, blocks_ref, turned_ref, factor_ref, factor_t_ref, a_ref, b_ref, cross_ref):
-    a_ref[...] = jnp.zeros_like(a_ref)
-    b_ref[...] = jnp.zeros_like(b_ref)
+def coefficients_kernel(panels, inner_ref, factor_ref, a_out, b_out, a_ref, b_ref, blocks_ref, turned_ref, cross_ref):
+    nb = factor_ref.shape[1]
+
+    def dot(left, right, dims=NN):
+        return dot_split(split(left), split(right), dims)
+
+    def place(p, i):
+        return slice(p * nb, (p + 1) * nb), slice(i * nb, (i + 1) * nb)
+
     for p in range(panels):
+        for i in range(panels):
+            block = inner_ref[place(p, i)]
+            if p > i:
+                blocks_ref[p, i] = block
+            else:
+                turned_ref[i, p] = block.T
+    a_out[...] = jnp.zeros_like(a_out)
+    b_out[...] = jnp.zeros_like(b_out)
+    for p in range(panels):
+        factor_t = factor_ref[p].T
         inner = turned_ref[p, p]
         for q in range(p):
             total = None
             for i in range(q + 1):
-                term = dot_full(turned_ref[p, i], a_ref[q, i], NT) + dot_full(blocks_ref[p, i], b_ref[q, i], NT)
+                term = dot(turned_ref[p, i], a_ref[q, i], NT) + dot(blocks_ref[p, i], b_ref[q, i], NT)
                 total = term if total is None else total + term
             cross_ref[q] = total
-            inner = inner - (dot_full(blocks_ref[p, q], total, NT) + dot_full(total, blocks_ref[p, q], NT))
+            inner = inner - (dot(blocks_ref[p, q], total, NT) + dot(total, blocks_ref[p, q], NT))
         for i in range(p):
             a_sum, b_sum = None, None
             for q in range(i, p):
-                term = dot_full(blocks_ref[p, q], a_ref[q, i])
+                term = dot(blocks_ref[p, q], a_ref[q, i])
                 a_sum = term if a_sum is None else a_sum + term
-                term = dot_full(blocks_ref[p, q], b_ref[q, i])
+                term = dot(blocks_ref[p, q], b_ref[q, i])
                 b_sum = term if b_sum is None else b_sum + term
-            a_ref[p, i] = -dot_full(factor_t_ref[p], a_sum)
-            b_ref[p, i] = -dot_full(factor_t_ref[p], cross_ref[i] + b_sum)
-        a_ref[p, p] = factor_t_ref[p]
-        b_ref[p, p] = -0.5 * dot_full(factor_t_ref[p], dot_full(inner, factor_ref[p]))
+            a_ref[p, i] = -dot(factor_t, a_sum)
+            b_ref[p, i] = -dot(factor_t, cross_ref[i] + b_sum)
+        a_ref[p, p] = factor_t
+        b_ref[p, p] = -0.5 * dot(factor_t, dot(inner, factor_ref[p]))
+    for p in range(panels):
+        for i in range(p + 1):
+            a_out[place(p, i)] = a_ref[p, i]
+            b_out[place(p, i)] = b_ref[p, i]
 
 
 def coefficients(inner, factor):
     panels, nb, _ = factor.shape
-    size = -(-nb // LANES) * LANES
-    grown = ((0, size - nb),) * 2
-    blocks = inner.reshape(panels, nb, panels, nb).transpose(0, 2, 1, 3)
-    blocks = jnp.pad(blocks, ((0, 0), (0, 0)) + grown)
-    factor = jnp.pad(factor, ((0, 0),) + grown)
-    shape = jax.ShapeDtypeStruct((panels, panels, size, size), F32)
-    a, b = pl.pallas_call(
+    shape = jax.ShapeDtypeStruct(inner.shape, F32)
+    return pl.pallas_call(
         functools.partial(coefficients_kernel, panels),
         out_shape=[shape, shape],
-        in_specs=[pl.BlockSpec(memory_space=pltpu.VMEM)] * 4,
-        scratch_shapes=[pltpu.VMEM((panels, size, size), F32)],
-        compiler_params=pltpu.CompilerParams(vmem_limit_bytes=VMEM_LIMIT),
+        in_specs=[pl.BlockSpec(memory_space=pltpu.VMEM)] * 2,
+        scratch_shapes=[pltpu.VMEM((panels, panels, nb, nb), F32)] * 4 + [pltpu.VMEM((panels, nb, nb), F32)],
+        compiler_params=params(),
         name="coefficients",
-    )(blocks, blocks.transpose(1, 0, 3, 2), factor, factor.transpose(0, 2, 1))
-    whole = lambda value: value[..., :nb, :nb].transpose(0, 2, 1, 3).reshape(panels * nb, panels * nb)
-    return whole(a), whole(b)
+    )(inner, factor)
 
 
 def update_kernel(count, pieces, width, table, a_ref, b_ref, m_ref, *refs):
@@ -357,7 +366,6 @@
     around = [own]
     for _ in range(row_count - 1):
         around.append(ring_shift(around[-1], ring))
-    around, far = lax.optimization_barrier((around, far))
     vcs = []
     for k in range(row_count):
         target = [(j % row_count + k) % row_count * per_row + j // row_count for j in range(col_count)]
@@ -367,7 +375,8 @@
             piece = jnp.where(wanted == i, around[i], piece)
         vcs.append(lax.ppermute(piece, "col", list(enumerate(target))))
 
-    partial = product_columns(table, near + far, symmetric, row_count)
+    partial = product_columns(table, 0, near, symmetric, row_count)
+    partial = product_columns(table, pairs, far, symmetric, row_count, partial)
     partial, vcs = lax.optimization_barrier((partial, vcs))
 
     total = partial[0]
@@ -388,7 +397,9 @@
     total = mine[0]
     for i in range(1, pairs):
         total = total + exchange(mine[i], offsets[i], col_count)
-    near_rows = [total] + [exchange(total, offset, col_count) for offset in offsets[1:pairs]]
+    near_rows = [total]
+    for i in range(1, pairs):
+        near_rows.append(exchange(total, offsets[i], col_count))
     far_rows = [exchange(piece, 1, col_count) for piece in near_rows]
 
     return update_matrix(table, a, b, vcs, pcs, near + far, near_rows + far_rows, symmetric)

time: 282 us -> 272 us (0.965)
  local copies, waits for them, and re-layouts: 19.2 us -> 11.5 us
  waiting for transfers between devices: 94.5 us -> 90.8 us
    ppermute x3, waiting for transfers between devices: 3.48 us -> 10.7 us  [total_over_all(): lax.ppermute(mine, 'row', [(i, (i + shift) % row_count) for i in range(ro...]
    pallas_call x1, Pallas kernels: 12.4 us -> 5.43 us  [coefficients(): pl.pallas_call(functools.partial(coefficients_kernel, panels), out_shape=...]
    pallas_call x1 -> x2, Pallas kernels: 26.3 us -> 32.7 us  [product_columns(): pl.pallas_call(functools.partial(columns_kernel, count, pieces, width, le...]
    ppermute x9, waiting for transfers between devices: 50 us -> 44.3 us  [ring_shift(): lax.ppermute(value, 'row', [(ring[i], ring[(i + 1) % size]) for i in rang...]
    ppermute x22, waiting for transfers between devices: 41 us -> 35.7 us  [exchange(): return lax.ppermute(value, 'col', [(i, i ^ offset) for i in range(count)])]
    transpose x6 -> x0, local copies, waits for them, and re-layouts: 3.72 us -> none  [the longest x4 1.89 us: coefficients(): value[..., :nb, :nb].transpose(0, 2, 1, 3).reshape(panels * nb, panels * nb)]
  transfers between devices with their start and end apart: 38 -> 38, of which waited for: 12 -> 14; matrix products, arithmetic and copies ran while one was open for 7% -> 5% of each run, Pallas kernels for 21% -> 21%
where the time goes in v2:
time: 272 us; the launch traced here: 271 us
  Pallas kernels  113 us (42%)
  waiting for transfers between devices  90.8 us (33%)
  starting transfers between devices  42.4 us (16%)
  local copies, waits for them, and re-layouts  11.5 us (4%)
  between operations  6.65 us (2%)
  other arithmetic  6.46 us (2%)
    ppermute x9, waiting for transfers between devices, ring_shift(): lax.ppermute(value, 'row', [(ring[i], ring[(i + 1) % size]) for i in rang...  44.3 us
    pallas_call x1, Pallas kernels, update_matrix(): pl.pallas_call(functools.partial(update_kernel, count, pieces, width), ou...  41.4 us
    ppermute x22, waiting for transfers between devices, exchange(): return lax.ppermute(value, 'col', [(i, i ^ offset) for i in range(count)])  35.7 us
    pallas_call x2, Pallas kernels, product_columns(): pl.pallas_call(functools.partial(columns_kernel, count, pieces, width, le...  32.7 us
    pallas_call x2, Pallas kernels, product_rows(): pl.pallas_call(functools.partial(rows_kernel, pieces, width, len(before))...  28.2 us
    ppermute x22, starting transfers between devices, exchange(): return lax.ppermute(value, 'col', [(i, i ^ offset) for i in range(count)])  17.1 us
    ppermute x9, starting transfers between devices, ring_shift(): lax.ppermute(value, 'row', [(ring[i], ring[(i + 1) % size]) for i in rang...  11.8 us
    ppermute x3, waiting for transfers between devices, total_over_all(): lax.ppermute(mine, 'row', [(i, (i + shift) % row_count) for i in range(ro...  10.7 us
  transfers between devices with their start and end apart: 38, of which 14 were waited for; matrix products, arithmetic and copies ran while one was open for 5% of the time, Pallas kernels for 21%

profile of v2, /device:TPU:0, one launch (start us, length us, event | category | flops | bytes accessed | tf_op | source)
XLA Modules:
  0.0 270.8 jit_solution(903514841461942616)
XLA Ops:
  0.0 3.1 %collective-permute-start.7 = (f32[256,512]{1,0:T(8,128)}, f32[256,512]{1,0:T(8,128)}, u32[]{:S(2)}, u32[]{:S(2)}) collective-permute-start(f32[256,512]{1,0:T(8,128)} %bitcast.40), channel_id=1, source_target_pairs={{0,8},{8,24},{24,16},{16,0},{1,9},{9,25},{25,17},{17,1},{2,10},{10... | collective-permute-start | bytes 1572872 | tf_op jit(solution)/shard_map/ppermute | solution.py:49
  3.1 2.4 collective-permute-start.5
  17.5 2.6 collective-permute-start.8
  21.6 7.1 %collective-permute-done.3.refs_2_.refs_10_ = f32[256,512]{1,0:T(8,128)S(1)} collective-permute-done((f32[256,512]{1,0:T(8,128)}, f32[256,512]{1,0:T(8,128)S(1)}, u32[]{:S(2)}, u32[]{:S(2)}) %collective-permute-start.3) | collective-permute-done | bytes 524320 | tf_op jit(solution)/shard_map/ppermute | solution.py:44
  29.3 3.8 %collective-permute-done.8 = f32[256,512]{1,0:T(8,128)} collective-permute-done((f32[256,512]{1,0:T(8,128)}, f32[256,512]{1,0:T(8,128)}, u32[]{:S(2)}, u32[]{:S(2)}) %collective-permute-start.8) | collective-permute-done | bytes 524320 | tf_op jit(solution)/shard_map/ppermute | solution.py:49
  33.1 1.7 collective-permute-start.9
  34.8 16.0 %product_columns.2 = (f32[256,512]{1,0:T(8,128)}, f32[256,512]{1,0:T(8,128)}, f32[256,512]{1,0:T(8,128)}, f32[256,512]{1,0:T(8,128)}) custom-call(s32[6,8]{1,0:T(8,128)} %stack.27.table, f32[256,512]{1,0:T(8,128)} %bitcast.45, f32[256,512]{1,0:T(8,128)} %copy-done.12, f32[256,512]{1,0:T(8,128)} %copy-done.11, f32[256,512]{1,0:T(8,128)} %copy-done.10, ...), custom_call_target="tpu_custom_call" | custom-call | flops 6442450944 | bytes 16777216 | tf_op jit(solution)/shard_map/product_columns/pallas_call | solution.py:91
  50.8 2.8 %select_select_fusion = (f32[256,512]{1,0:T(8,128)}, f32[256,512]{1,0:T(8,128)}, f32[256,512]{1,0:T(8,128)}, f32[256,512]{1,0:T(8,128)}) fusion(f32[256,512]{1,0:T(8,128)S(1)} %collective-permute-done.9, f32[256,512]{1,0:T(8,128)} %collective-permute-done.8, f32[256,512]{1,0:T(8,128)} %collective-permute-done.7, pred[]{:T(512)S(6)} %eq.72, pred[]{:T(512)S(6)} %eq.71, ...), kind=kLoop, calls=%fused_computation.9 | loop fusion | flops 1572864 | bytes 4194316 | tf_op jit(solution)/shard_map/jit(_where)/select_n | solution.py:375
  53.6 4.3 %collective-permute-start.13 = (f32[256,512]{1,0:T(8,128)}, f32[256,512]{1,0:T(8,128)S(1)}, u32[]{:S(2)}, u32[]{:S(2)}) collective-permute-start(f32[256,512]{1,0:T(8,128)} %get-tuple-element.44), channel_id=1, source_target_pairs={{0,6},{1,0},{2,2},{3,4},{4,7},{5,1},{6,3},{7,5},{8,14},{9,8},{10,1... | collective-permute-start | bytes 1572872 | tf_op jit(solution)/shard_map/ppermute | solution.py:376
  59.0 3.8 %collective-permute-start.11 = (f32[256,512]{1,0:T(8,128)}, f32[256,512]{1,0:T(8,128)S(1)}, u32[]{:S(2)}, u32[]{:S(2)}) collective-permute-start(f32[256,512]{1,0:T(8,128)} %get-tuple-element.46), channel_id=1, source_target_pairs={{0,2},{1,4},{2,6},{3,0},{4,3},{5,5},{6,7},{7,1},{8,10},{9,12},{10,... | collective-permute-start | bytes 1572872 | tf_op jit(solution)/shard_map/ppermute | solution.py:376
  62.8 1.7 collective-permute-start.10
  64.5 16.7 %product_columns.3 = (f32[256,512]{1,0:T(8,128)}, f32[256,512]{1,0:T(8,128)}, f32[256,512]{1,0:T(8,128)}, f32[256,512]{1,0:T(8,128)}) custom-call(s32[6,8]{1,0:T(8,128)} %stack.27.table, f32[256,512]{1,0:T(8,128)} %copy-done.13, f32[256,512]{1,0:T(8,128)} %collective-permute-done.2.refs_1_.refs_13_, f32[256,512]{1,0:T(8,128)} %collective-permute-done.4.refs_2_.refs_14_, ...), custom_call_target="tpu_custom_call" | custom-call | flops 6442450944 | bytes 16777216 | tf_op jit(solution)/shard_map/product_columns/pallas_call | solution.py:91
  82.6 14.0 %product_rows.2 = f32[4,512,256]{2,1,0:T(8,128)} custom-call(s32[6,8]{1,0:T(8,128)} %stack.27.table, f32[256,512]{1,0:T(8,128)} %copy-done.3, f32[256,512]{1,0:T(8,128)} %copy-done.2, f32[256,512]{1,0:T(8,128)} %copy-done.1, f32[256,512]{1,0:T(8,128)} %copy-done, f32[4096,2048]{1,0:T(8,128)} %m_ref.1), custom_call_target="tpu_custom_call" | custom-call | flops 6442450944 | bytes 16777216 | tf_op jit(solution)/shard_map/product_rows/pallas_call | solution.py:136
  98.4 13.5 %collective-permute-done.21 = f32[256,512]{1,0:T(8,128)S(1)} collective-permute-done((f32[256,512]{1,0:T(8,128)S(1)}, f32[256,512]{1,0:T(8,128)S(1)}, u32[]{:S(2)}, u32[]{:S(2)}) %collective-permute-start.21) | collective-permute-done | bytes 524320 | tf_op jit(solution)/shard_map/ppermute | solution.py:49
  112.5 13.6 %collective-permute-done.22 = f32[256,512]{1,0:T(8,128)S(1)} collective-permute-done((f32[256,512]{1,0:T(8,128)S(1)}, f32[256,512]{1,0:T(8,128)S(1)}, u32[]{:S(2)}, u32[]{:S(2)}) %collective-permute-start.22) | collective-permute-done | bytes 524320 | tf_op jit(solution)/shard_map/ppermute | solution.py:49
  126.2 5.2 %inner_products.1 = f32[256,256]{1,0:T(8,128)} custom-call(s32[6,8]{1,0:T(8,128)} %stack.27.table, f32[256,512]{1,0:T(8,128)} %bitcast.46, f32[256,512]{1,0:T(8,128)} %copy-done.3, f32[256,512]{1,0:T(8,128)} %copy-done.2, f32[256,512]{1,0:T(8,128)} %copy-done.1, f32[256,512]{1,0:T(8,128)} %copy-done, f32[256,512]{1,0:T(8,128)} %get-tuple-element.35.refs_4_, ...), custom_call_target="tpu_custom_call" | custom-call | flops 1006632960 | bytes 4194304 | tf_op jit(solution)/shard_map/inner_products/pallas_call | solution.py:177
  131.5 7.8 %collective-permute-done.23 = f32[256,512]{1,0:T(8,128)S(1)} collective-permute-done((f32[256,512]{1,0:T(8,128)S(1)}, f32[256,512]{1,0:T(8,128)S(1)}, u32[]{:S(2)}, u32[]{:S(2)}) %collective-permute-start.23) | collective-permute-done | bytes 524320 | tf_op jit(solution)/shard_map/ppermute | solution.py:49
  141.0 14.2 %product_rows.3 = f32[4,512,256]{2,1,0:T(8,128)} custom-call(s32[6,8]{1,0:T(8,128)} %stack.27.table, f32[256,512]{1,0:T(8,128)} %copy-done.3, f32[256,512]{1,0:T(8,128)} %copy-done.2, f32[256,512]{1,0:T(8,128)} %copy-done.1, f32[256,512]{1,0:T(8,128)} %copy-done, f32[4096,2048]{1,0:T(8,128)} %m_ref.1, f32[4,512,256]{2,1,0:T(8,128)} %copy-done.5), custom_call_target="tpu_custom_call" | custom-call | flops 6442450944 | bytes 16777216 | tf_op jit(solution)/shard_map/product_rows/pallas_call | solution.py:136
  155.3 2.6 slice_bitcast_fusion.2
  157.9 2.8 %collective-permute-start.28 = (f32[512,256]{1,0:T(8,128)}, f32[512,256]{1,0:T(8,128)S(1)}, u32[]{:S(2)}, u32[]{:S(2)}) collective-permute-start(f32[512,256]{1,0:T(8,128)} %get-tuple-element.41), channel_id=1, source_target_pairs={{0,2},{1,3},{2,0},{3,1},{4,6},{5,7},{6,4},{7,5},{8,10},{9,11},{10,... | collective-permute-start | bytes 1572872 | tf_op jit(solution)/shard_map/ppermute | solution.py:44
  162.2 2.1 collective-permute-start.15
  164.3 20.7 %collective-permute-done.15 = f32[128,256]{1,0:T(8,128)S(1)} collective-permute-done((f32[128,256]{1,0:T(8,128)S(1)}, f32[128,256]{1,0:T(8,128)S(1)}, u32[]{:S(2)}, u32[]{:S(2)}) %collective-permute-start.15) | collective-permute-done | bytes 131104 | tf_op jit(solution)/shard_map/ppermute | solution.py:44
  186.4 3.6 %collective-permute-done.16 = f32[128,256]{1,0:T(8,128)S(1)} collective-permute-done((f32[128,256]{1,0:T(8,128)S(1)}, f32[128,256]{1,0:T(8,128)S(1)}, u32[]{:S(2)}, u32[]{:S(2)}) %collective-permute-start.16) | collective-permute-done | bytes 131104 | tf_op jit(solution)/shard_map/ppermute | solution.py:44
  190.0 1.9 collective-permute-start.19
  191.9 1.7 collective-permute-start.18
  195.9 2.5 collective-permute-start.33
  199.7 2.5 collective-permute-done.18
  202.2 8.2 %collective-permute-done.17 = f32[128,256]{1,0:T(8,128)S(1)} collective-permute-done((f32[128,256]{1,0:T(8,128)S(1)}, f32[128,256]{1,0:T(8,128)S(1)}, u32[]{:S(2)}, u32[]{:S(2)}) %collective-permute-start.17) | collective-permute-done | bytes 131104 | tf_op jit(solution)/shard_map/ppermute | solution.py:320
  214.1 2.9 %collective-permute-done.32.refs_18_ = f32[512,256]{1,0:T(8,128)S(1)} collective-permute-done((f32[512,256]{1,0:T(8,128)S(1)}, f32[512,256]{1,0:T(8,128)S(1)}, u32[]{:S(2)}, u32[]{:S(2)}) %collective-permute-start.32) | collective-permute-done | bytes 524320 | tf_op jit(solution)/shard_map/ppermute | solution.py:44
  218.2 5.4 %coefficients.1 = (f32[256,256]{1,0:T(8,128)}, f32[256,256]{1,0:T(8,128)}) custom-call(f32[256,256]{1,0:T(8,128)} %pad_maximum_fusion.inner_ref, f32[4,64,64]{2,1,0:T(8,128)} %factor_ref.1), custom_call_target="tpu_custom_call" | custom-call | tf_op jit(solution)/shard_map/coefficients/pallas_call | solution.py:236
  223.7 4.8 %collective-permute-done.26.refs_7_ = f32[256,512]{1,0:T(8,128)} collective-permute-done((f32[256,512]{1,0:T(8,128)S(1)}, f32[256,512]{1,0:T(8,128)}, u32[]{:S(2)}, u32[]{:S(2)}) %collective-permute-start.26) | collective-permute-done | bytes 524320 | tf_op jit(solution)/shard_map/ppermute | solution.py:49
  229.3 41.4 %update_matrix.1 = f32[4096,2048]{1,0:T(8,128)} custom-call(s32[6,8]{1,0:T(8,128)} %stack.27.table, f32[256,256]{1,0:T(8,128)} %get-tuple-element.39.a_ref, f32[256,256]{1,0:T(8,128)} %get-tuple-element.40.b_ref, f32[4096,2048]{1,0:T(8,128)} %m_ref.1, f32[256,512]{1,0:T(8,128)} %copy-done.3, f32[256,512]{1,0:T(8,128)} %copy-done.2, f32[256,512]{1,0:T(8,128)} %copy-done.1, ...), custom_call_target="tpu_custom_call" | custom-call | flops 25769803776 | bytes 67108864 | tf_op jit(solution)/shard_map/update_matrix/pallas_call | solution.py:287
  (123 shorter events, 26.6 us)
Async XLA Ops:
  0.0 17.5 %collective-permute-start.7 = (f32[256,512]{1,0:T(8,128)}, f32[256,512]{1,0:T(8,128)}, u32[]{:S(2)}, u32[]{:S(2)}) collective-permute-start(f32[256,512]{1,0:T(8,128)} %bitcast.40), channel_id=1, source_target_pairs={{0,8},{8,24},{24,16},{16,0},{1,9},{9,25},{25,17},{17,1},{2,10},{10... | collective-permute-start | bytes 1572872 | tf_op jit(solution)/shard_map/ppermute | solution.py:49
  3.1 18.4 %collective-permute-start.5 = (f32[256,512]{1,0:T(8,128)}, f32[256,512]{1,0:T(8,128)S(1)}, u32[]{:S(2)}, u32[]{:S(2)}) collective-permute-start(f32[256,512]{1,0:T(8,128)} %bitcast.41), channel_id=1, source_target_pairs={{0,6},{1,7},{2,4},{3,5},{4,2},{5,3},{6,0},{7,1},{8,14},{9,15},{10,... | collective-permute-start | bytes 1572872 | tf_op jit(solution)/shard_map/ppermute | solution.py:44
  5.5 23.3 %collective-permute-start.3 = (f32[256,512]{1,0:T(8,128)}, f32[256,512]{1,0:T(8,128)S(1)}, u32[]{:S(2)}, u32[]{:S(2)}) collective-permute-start(f32[256,512]{1,0:T(8,128)} %bitcast.42), channel_id=1, source_target_pairs={{0,4},{1,5},{2,6},{3,7},{4,0},{5,1},{6,2},{7,3},{8,12},{9,13},{10,... | collective-permute-start | bytes 1572872 | tf_op jit(solution)/shard_map/ppermute | solution.py:44
  6.0 22.9 %collective-permute-start.1 = (f32[256,512]{1,0:T(8,128)}, f32[256,512]{1,0:T(8,128)S(1)}, u32[]{:S(2)}, u32[]{:S(2)}) collective-permute-start(f32[256,512]{1,0:T(8,128)} %bitcast.43), channel_id=1, source_target_pairs={{0,2},{1,3},{2,0},{3,1},{4,6},{5,7},{6,4},{7,5},{8,10},{9,11},{10,... | collective-permute-start | bytes 1572872 | tf_op jit(solution)/shard_map/ppermute | solution.py:44
  6.5 51.4 %collective-permute-start = (f32[256,512]{1,0:T(8,128)}, f32[256,512]{1,0:T(8,128)S(1)}, u32[]{:S(2)}, u32[]{:S(2)}) collective-permute-start(f32[256,512]{1,0:T(8,128)} %bitcast.44), channel_id=1, source_target_pairs={{0,1},{1,0},{2,3},{3,2},{4,5},{5,4},{6,7},{7,6},{8,9},{9,8},{10,11... | collective-permute-start | bytes 1572872 | tf_op jit(solution)/shard_map/ppermute | solution.py:44
  17.5 15.6 %collective-permute-start.8 = (f32[256,512]{1,0:T(8,128)}, f32[256,512]{1,0:T(8,128)}, u32[]{:S(2)}, u32[]{:S(2)}) collective-permute-start(f32[256,512]{1,0:T(8,128)} %collective-permute-done.7), channel_id=1, source_target_pairs={{0,8},{8,24},{24,16},{16,0},{1,9},{9,25},{25,17},{17,1},{2,10},{10... | collective-permute-start | bytes 1572872 | tf_op jit(solution)/shard_map/ppermute | solution.py:49
  21.4 36.6 %collective-permute-start.6 = (f32[256,512]{1,0:T(8,128)S(1)}, f32[256,512]{1,0:T(8,128)S(1)}, u32[]{:S(2)}, u32[]{:S(2)}) collective-permute-start(f32[256,512]{1,0:T(8,128)S(1)} %collective-permute-done.5.refs_3_.refs_11_), channel_id=1, source_target_pairs={{0,1},{1,0},{2,3},{3,2},{4,5},{5,4},{6,7},{7,6},{8,9},{9,8},{10,11... | collective-permute-start | bytes 1572872 | tf_op jit(solution)/shard_map/ppermute | solution.py:44
  28.8 34.0 %collective-permute-start.4 = (f32[256,512]{1,0:T(8,128)S(1)}, f32[256,512]{1,0:T(8,128)}, u32[]{:S(2)}, u32[]{:S(2)}) collective-permute-start(f32[256,512]{1,0:T(8,128)S(1)} %collective-permute-done.3.refs_2_.refs_10_), channel_id=1, source_target_pairs={{0,1},{1,0},{2,3},{3,2},{4,5},{5,4},{6,7},{7,6},{8,9},{9,8},{10,11... | collective-permute-start | bytes 1572872 | tf_op jit(solution)/shard_map/ppermute | solution.py:44
  28.9 35.6 %collective-permute-start.2 = (f32[256,512]{1,0:T(8,128)S(1)}, f32[256,512]{1,0:T(8,128)}, u32[]{:S(2)}, u32[]{:S(2)}) collective-permute-start(f32[256,512]{1,0:T(8,128)S(1)} %collective-permute-done.1.refs_1_.refs_9_), channel_id=1, source_target_pairs={{0,1},{1,0},{2,3},{3,2},{4,5},{5,4},{6,7},{7,6},{8,9},{9,8},{10,11... | collective-permute-start | bytes 1572872 | tf_op jit(solution)/shard_map/ppermute | solution.py:44
  33.1 17.7 %collective-permute-start.9 = (f32[256,512]{1,0:T(8,128)}, f32[256,512]{1,0:T(8,128)S(1)}, u32[]{:S(2)}, u32[]{:S(2)}) collective-permute-start(f32[256,512]{1,0:T(8,128)} %collective-permute-done.8), channel_id=1, source_target_pairs={{0,8},{8,24},{24,16},{16,0},{1,9},{9,25},{25,17},{17,1},{2,10},{10... | collective-permute-start | bytes 1572872 | tf_op jit(solution)/shard_map/ppermute | solution.py:49
  53.6 27.6 %collective-permute-start.13 = (f32[256,512]{1,0:T(8,128)}, f32[256,512]{1,0:T(8,128)S(1)}, u32[]{:S(2)}, u32[]{:S(2)}) collective-permute-start(f32[256,512]{1,0:T(8,128)} %get-tuple-element.44), channel_id=1, source_target_pairs={{0,6},{1,0},{2,2},{3,4},{4,7},{5,1},{6,3},{7,5},{8,14},{9,8},{10,1... | collective-permute-start | bytes 1572872 | tf_op jit(solution)/shard_map/ppermute | solution.py:376
  58.0 23.2 %collective-permute-start.12 = (f32[256,512]{1,0:T(8,128)}, f32[256,512]{1,0:T(8,128)S(1)}, u32[]{:S(2)}, u32[]{:S(2)}) collective-permute-start(f32[256,512]{1,0:T(8,128)} %get-tuple-element.45), channel_id=1, source_target_pairs={{0,4},{1,6},{2,0},{3,2},{4,5},{5,7},{6,1},{7,3},{8,12},{9,14},{10,... | collective-permute-start | bytes 1572872 | tf_op jit(solution)/shard_map/ppermute | solution.py:376
  59.0 22.4 %collective-permute-start.11 = (f32[256,512]{1,0:T(8,128)}, f32[256,512]{1,0:T(8,128)S(1)}, u32[]{:S(2)}, u32[]{:S(2)}) collective-permute-start(f32[256,512]{1,0:T(8,128)} %get-tuple-element.46), channel_id=1, source_target_pairs={{0,2},{1,4},{2,6},{3,0},{4,3},{5,5},{6,7},{7,1},{8,10},{9,12},{10,... | collective-permute-start | bytes 1572872 | tf_op jit(solution)/shard_map/ppermute | solution.py:376
  62.8 18.6 %collective-permute-start.10 = (f32[256,512]{1,0:T(8,128)}, f32[256,512]{1,0:T(8,128)S(1)}, u32[]{:S(2)}, u32[]{:S(2)}) collective-permute-start(f32[256,512]{1,0:T(8,128)} %get-tuple-element.47), channel_id=1, source_target_pairs={{0,0},{1,2},{2,4},{3,6},{4,1},{5,3},{6,5},{7,7},{8,8},{9,10},{10,1... | collective-permute-start | bytes 1572872 | tf_op jit(solution)/shard_map/ppermute | solution.py:376
  96.6 43.1 %collective-permute-start.27 = (f32[4,512,256]{2,1,0:T(8,128)}, f32[4,512,256]{2,1,0:T(8,128)S(1)}, u32[]{:S(2)}, u32[]{:S(2)}) collective-permute-start(f32[4,512,256]{2,1,0:T(8,128)} %product_rows.2), channel_id=1, source_target_pairs={{0,1},{1,0},{2,3},{3,2},{4,5},{5,4},{6,7},{7,6},{8,9},{9,8},{10,11... | collective-permute-start | bytes 6291464 | tf_op jit(solution)/shard_map/ppermute | solution.py:44
  97.0 14.9 %collective-permute-start.21 = (f32[256,512]{1,0:T(8,128)S(1)}, f32[256,512]{1,0:T(8,128)S(1)}, u32[]{:S(2)}, u32[]{:S(2)}) collective-permute-start(f32[256,512]{1,0:T(8,128)S(1)} %copy-done.17), channel_id=1, source_target_pairs={{0,8},{8,24},{24,16},{16,0},{1,9},{9,25},{25,17},{17,1},{2,10},{10... | collective-permute-start | bytes 1572872 | tf_op jit(solution)/shard_map/ppermute | solution.py:49
  112.0 14.1 %collective-permute-start.22 = (f32[256,512]{1,0:T(8,128)S(1)}, f32[256,512]{1,0:T(8,128)S(1)}, u32[]{:S(2)}, u32[]{:S(2)}) collective-permute-start(f32[256,512]{1,0:T(8,128)S(1)} %add.197), channel_id=1, source_target_pairs={{0,8},{8,24},{24,16},{16,0},{1,9},{9,25},{25,17},{17,1},{2,10},{10... | collective-permute-start | bytes 1572872 | tf_op jit(solution)/shard_map/ppermute | solution.py:49
  126.1 13.2 %collective-permute-start.23 = (f32[256,512]{1,0:T(8,128)S(1)}, f32[256,512]{1,0:T(8,128)S(1)}, u32[]{:S(2)}, u32[]{:S(2)}) collective-permute-start(f32[256,512]{1,0:T(8,128)S(1)} %add.198), channel_id=1, source_target_pairs={{0,8},{8,24},{24,16},{16,0},{1,9},{9,25},{25,17},{17,1},{2,10},{10... | collective-permute-start | bytes 1572872 | tf_op jit(solution)/shard_map/ppermute | solution.py:49
  131.4 30.7 %collective-permute-start.14 = (f32[256,256]{1,0:T(8,128)}, f32[256,256]{1,0:T(8,128)S(1)}, u32[]{:S(2)}, u32[]{:S(2)}) collective-permute-start(f32[256,256]{1,0:T(8,128)} %inner_products.1), channel_id=1, source_target_pairs={{0,1},{1,0},{2,3},{3,2},{4,5},{5,4},{6,7},{7,6},{8,9},{9,8},{10,11... | collective-permute-start | bytes 786440 | tf_op jit(solution)/shard_map/ppermute | solution.py:44
  139.4 52.5 %collective-permute-start.24 = (f32[256,512]{1,0:T(8,128)S(1)}, f32[256,512]{1,0:T(8,128)}, u32[]{:S(2)}, u32[]{:S(2)}) collective-permute-start(f32[256,512]{1,0:T(8,128)S(1)} %add.199.refs_4_), channel_id=1, source_target_pairs={{0,8},{8,24},{24,16},{16,0},{1,9},{9,25},{25,17},{17,1},{2,10},{10... | collective-permute-start | bytes 1572872 | tf_op jit(solution)/shard_map/ppermute | solution.py:49
  157.9 35.8 %collective-permute-start.28 = (f32[512,256]{1,0:T(8,128)}, f32[512,256]{1,0:T(8,128)S(1)}, u32[]{:S(2)}, u32[]{:S(2)}) collective-permute-start(f32[512,256]{1,0:T(8,128)} %get-tuple-element.41), channel_id=1, source_target_pairs={{0,2},{1,3},{2,0},{3,1},{4,6},{5,7},{6,4},{7,5},{8,10},{9,11},{10,... | collective-permute-start | bytes 1572872 | tf_op jit(solution)/shard_map/ppermute | solution.py:44
  160.7 34.0 %collective-permute-start.30 = (f32[512,256]{1,0:T(8,128)}, f32[512,256]{1,0:T(8,128)S(1)}, u32[]{:S(2)}, u32[]{:S(2)}) collective-permute-start(f32[512,256]{1,0:T(8,128)} %get-tuple-element.42), channel_id=1, source_target_pairs={{0,6},{1,7},{2,4},{3,5},{4,2},{5,3},{6,0},{7,1},{8,14},{9,15},{10,... | collective-permute-start | bytes 1572872 | tf_op jit(solution)/shard_map/ppermute | solution.py:44
  161.8 33.0 %collective-permute-start.29 = (f32[512,256]{1,0:T(8,128)}, f32[512,256]{1,0:T(8,128)S(1)}, u32[]{:S(2)}, u32[]{:S(2)}) collective-permute-start(f32[512,256]{1,0:T(8,128)} %get-tuple-element.43), channel_id=1, source_target_pairs={{0,4},{1,5},{2,6},{3,7},{4,0},{5,1},{6,2},{7,3},{8,12},{9,13},{10,... | collective-permute-start | bytes 1572872 | tf_op jit(solution)/shard_map/ppermute | solution.py:44
  162.2 22.8 %collective-permute-start.15 = (f32[128,256]{1,0:T(8,128)S(1)}, f32[128,256]{1,0:T(8,128)S(1)}, u32[]{:S(2)}, u32[]{:S(2)}) collective-permute-start(f32[128,256]{1,0:T(8,128)S(1)} %dynamic-slice_add_fusion), channel_id=1, source_target_pairs={{0,2},{1,3},{2,0},{3,1},{4,6},{5,7},{6,4},{7,5},{8,10},{9,11},{10,... | collective-permute-start | bytes 393224 | tf_op jit(solution)/shard_map/ppermute | solution.py:44
  193.7 19.2 %collective-permute-start.25 = (f32[256,512]{1,0:T(8,128)}, f32[256,512]{1,0:T(8,128)S(1)}, u32[]{:S(2)}, u32[]{:S(2)}) collective-permute-start(f32[256,512]{1,0:T(8,128)} %collective-permute-done.24.refs_5_), channel_id=1, source_target_pairs={{0,8},{8,24},{24,16},{16,0},{1,9},{9,25},{25,17},{17,1},{2,10},{10... | collective-permute-start | bytes 1572872 | tf_op jit(solution)/shard_map/ppermute | solution.py:49
  195.9 18.1 %collective-permute-start.33 = (f32[512,256]{1,0:T(8,128)S(1)}, f32[512,256]{1,0:T(8,128)S(1)}, u32[]{:S(2)}, u32[]{:S(2)}) collective-permute-start(f32[512,256]{1,0:T(8,128)S(1)} %fusion.2.refs_16_), channel_id=1, source_target_pairs={{0,6},{1,7},{2,4},{3,5},{4,2},{5,3},{6,0},{7,1},{8,14},{9,15},{10,... | collective-permute-start | bytes 1572872 | tf_op jit(solution)/shard_map/ppermute | solution.py:44
  198.5 18.5 %collective-permute-start.32 = (f32[512,256]{1,0:T(8,128)S(1)}, f32[512,256]{1,0:T(8,128)S(1)}, u32[]{:S(2)}, u32[]{:S(2)}) collective-permute-start(f32[512,256]{1,0:T(8,128)S(1)} %fusion.2.refs_16_), channel_id=1, source_target_pairs={{0,4},{1,5},{2,6},{3,7},{4,0},{5,1},{6,2},{7,3},{8,12},{9,13},{10,... | collective-permute-start | bytes 1572872 | tf_op jit(solution)/shard_map/ppermute | solution.py:44
  199.2 17.8 %collective-permute-start.31 = (f32[512,256]{1,0:T(8,128)S(1)}, f32[512,256]{1,0:T(8,128)S(1)}, u32[]{:S(2)}, u32[]{:S(2)}) collective-permute-start(f32[512,256]{1,0:T(8,128)S(1)} %fusion.2.refs_16_), channel_id=1, source_target_pairs={{0,2},{1,3},{2,0},{3,1},{4,6},{5,7},{6,4},{7,5},{8,10},{9,11},{10,... | collective-permute-start | bytes 1572872 | tf_op jit(solution)/shard_map/ppermute | solution.py:44
  211.9 16.6 %collective-permute-start.34 = (f32[512,256]{1,0:T(8,128)S(1)}, f32[512,256]{1,0:T(8,128)S(1)}, u32[]{:S(2)}, u32[]{:S(2)}) collective-permute-start(f32[512,256]{1,0:T(8,128)S(1)} %fusion.2.refs_16_), channel_id=1, source_target_pairs={{0,1},{1,0},{2,3},{3,2},{4,5},{5,4},{6,7},{7,6},{8,9},{9,8},{10,11... | collective-permute-start | bytes 1572872 | tf_op jit(solution)/shard_map/ppermute | solution.py:44
  212.8 15.6 %collective-permute-start.26 = (f32[256,512]{1,0:T(8,128)S(1)}, f32[256,512]{1,0:T(8,128)}, u32[]{:S(2)}, u32[]{:S(2)}) collective-permute-start(f32[256,512]{1,0:T(8,128)S(1)} %collective-permute-done.25.refs_6_), channel_id=1, source_target_pairs={{0,8},{8,24},{24,16},{16,0},{1,9},{9,25},{25,17},{17,1},{2,10},{10... | collective-permute-start | bytes 1572872 | tf_op jit(solution)/shard_map/ppermute | solution.py:49
  214.0 14.5 %collective-permute-start.37 = (f32[512,256]{1,0:T(8,128)S(1)}, f32[512,256]{1,0:T(8,128)}, u32[]{:S(2)}, u32[]{:S(2)}) collective-permute-start(f32[512,256]{1,0:T(8,128)S(1)} %collective-permute-done.33.refs_19_), channel_id=1, source_target_pairs={{0,1},{1,0},{2,3},{3,2},{4,5},{5,4},{6,7},{7,6},{8,9},{9,8},{10,11... | collective-permute-start | bytes 1572872 | tf_op jit(solution)/shard_map/ppermute | solution.py:44
  217.0 11.5 %collective-permute-start.36 = (f32[512,256]{1,0:T(8,128)S(1)}, f32[512,256]{1,0:T(8,128)}, u32[]{:S(2)}, u32[]{:S(2)}) collective-permute-start(f32[512,256]{1,0:T(8,128)S(1)} %collective-permute-done.32.refs_18_), channel_id=1, source_target_pairs={{0,1},{1,0},{2,3},{3,2},{4,5},{5,4},{6,7},{7,6},{8,9},{9,8},{10,11... | collective-permute-start | bytes 1572872 | tf_op jit(solution)/shard_map/ppermute | solution.py:44
  (29 other events, 322.6 us)
